TPU v7x, 512 devices: a whole 4x8x8 slice. The times are simulated.
512 devices in a mesh: seq: 32 (over x, y), exp: 16 (over z, core).
Axes of the slice: x: 4, y: 8, z: 8, core: 2. Of those that a mesh axis runs over, the one named last changes fastest.
Arguments:
- mixer_query: bfloat16 [16, 2048, 1024], P('exp', 'seq'), may hold values from -6 to 6
- mixer_key: bfloat16 [16, 2048, 1024], P('exp', 'seq'), may hold values from -6 to 6
- mixer_value: bfloat16 [16, 2048, 2048], P('exp', 'seq'), may hold values from -6 to 6
- log_decay: bfloat16 [16, 2048, 16], P('exp', 'seq'), may hold values from -0.75 to 0
- strength: bfloat16 [16, 2048, 16], P('exp', 'seq'), may hold values from 0 to 0.9
- residual: bfloat16 [16, 2048, 2048], P('exp', 'seq'), may hold values from -6 to 6
- out_gain: float32 [128], replicated, may hold values from 0.25 to 1.75
- ffn_gain: float32 [2048], replicated, may hold values from 0.25 to 1.75
- expert_ids: int32 [16, 2048, 10], P('exp', 'seq'), may hold values from 0 to 511, all different within a row; in each aligned block of 64 rows (0 to 63, 64 to 127, ..., all dimensions but the last counted through in order) at most 2 rows name the same one
- expert_weights: float32 [16, 2048, 10], P('exp', 'seq'), may hold values from 0.05 to 0.25
- gate_proj: bfloat16 [512, 2048, 256], P(('seq', 'exp')), may hold values from -0.125 to 0.125
- up_proj: bfloat16 [512, 2048, 256], P(('seq', 'exp')), may hold values from -0.125 to 0.125
- down_proj: bfloat16 [512, 256, 2048], P(('seq', 'exp')), may hold values from -0.375 to 0.375
Outputs:
- mixed: bfloat16 [16, 2048, 2048], P('exp', 'seq')
- ffn_out: bfloat16 [16, 2048, 2048], P('exp', 'seq')
Inputs may be any that keep to these rules, and one draw needn't show every extreme that they name: `expert_ids`: each row names 10 different experts; the 64 rows of one device (an aligned block) name no expert more than 2 times, and some block names an expert exactly 2 times.
All inputs are finite; a program needn't handle non-finite values.
Results may differ from a plain program's by a relative error of at most 0.018.
Values may be sent and summed in bfloat16 or wider, within the bound.
No kernel may reach another device: no remote copies, remote signals or barrier semaphores. Data moves between devices by JAX's collectives and lax.ppermute only.
A program may use at most 64 MiB of HBM per device.

v0:
```python
import jax
import jax.numpy as jnp
from jax import lax
from jax.sharding import PartitionSpec as P

D = 2048
DH = 128
HK = 8
VALUE_HEADS = 16
TOPK = 10
BLOCK = 64


def unit_rows(matrix):
    matrix = matrix.astype(jnp.float32)
    return matrix * lax.rsqrt(jnp.sum(matrix * matrix, axis=-1, keepdims=True) + 1e-06)


def block_parts(query_rows, key_rows, values, decay_rows, strength_rows):
    block_size = query_rows.shape[1]
    cumulative = jnp.cumsum(decay_rows, axis=1)
    spread = cumulative[:, :, None] - cumulative[:, None, :]
    row_index = lax.broadcasted_iota(jnp.int32, (block_size, block_size), 0)
    col_index = lax.broadcasted_iota(jnp.int32, (block_size, block_size), 1)
    strict_lower = row_index > col_index
    inclusive = row_index >= col_index
    fade_lower = jnp.where(strict_lower, jnp.exp(jnp.where(strict_lower, spread, 0.0)), 0.0)
    fade_inclusive = jnp.where(inclusive, jnp.exp(jnp.where(inclusive, spread, 0.0)), 0.0)
    key_dot = jnp.einsum("nik,njk->nij", key_rows, key_rows, precision=lax.Precision.HIGHEST)
    query_dot = jnp.einsum("nik,njk->nij", query_rows, key_rows, precision=lax.Precision.HIGHEST)
    negated = -(strength_rows[:, :, None] * key_dot * fade_lower)
    identity_block = jnp.eye(block_size, dtype=jnp.float32)
    inverse = identity_block + negated
    powered = negated
    for level_index in range(block_size.bit_length() - 2):
        powered = jnp.einsum("nij,njk->nik", powered, powered, precision=lax.Precision.HIGHEST)
        inverse = jnp.einsum(
            "nij,njk->nik", inverse, identity_block + powered, precision=lax.Precision.HIGHEST
        )
    decay_gain = jnp.exp(cumulative)
    last_total = cumulative[:, -1:]
    tail_gain = jnp.exp(last_total - cumulative)
    beta_keys = (strength_rows * decay_gain)[:, :, None] * key_rows
    weighted_keys = jnp.einsum("nij,njk->nik", inverse, beta_keys, precision=lax.Precision.HIGHEST)
    updated_value_rows = jnp.einsum(
        "nij,njk->nik", inverse, strength_rows[:, :, None] * values, precision=lax.Precision.HIGHEST
    )
    scores = query_dot * fade_inclusive
    query_part = decay_gain[:, :, None] * query_rows - jnp.einsum(
        "nij,njk->nik", scores, weighted_keys, precision=lax.Precision.HIGHEST
    )
    local_out = jnp.einsum(
        "nij,njk->nik", scores, updated_value_rows, precision=lax.Precision.HIGHEST
    )
    attenuated_keys = tail_gain[:, :, None] * key_rows
    key_identity = jnp.eye(key_rows.shape[2], dtype=jnp.float32)
    transition = jnp.exp(last_total)[:, :, None] * key_identity - jnp.einsum(
        "nck,ncl->nkl", attenuated_keys, weighted_keys, precision=lax.Precision.HIGHEST
    )
    inserted_signal = jnp.einsum(
        "wjf,wjd->wfd", attenuated_keys, updated_value_rows, precision=lax.Precision.HIGHEST
    )
    return (query_part, local_out, transition, inserted_signal)


def apply_map(matrix, carried):
    return jnp.einsum("lij,ljk->lik", matrix, carried, precision=lax.Precision.HIGHEST)


def body(
    mixer_query,
    mixer_key,
    mixer_value,
    log_decay,
    strength,
    residual,
    out_gain,
    ffn_gain,
    expert_ids,
    expert_weights,
    gate_proj,
    up_proj,
    down_proj,
):
    seq_devices = lax.axis_size("seq")
    exp_devices = lax.axis_size("exp")
    local_tokens = residual.shape[1]
    lane_total = max(VALUE_HEADS, seq_devices)
    lane_count = lane_total // seq_devices
    lane_width = VALUE_HEADS * DH // lane_total
    query_flat = jnp.repeat(
        mixer_query.reshape(local_tokens, HK, DH), lane_total // HK, axis=1
    ).reshape(local_tokens, lane_total * DH)
    key_flat = jnp.repeat(
        mixer_key.reshape(local_tokens, HK, DH), lane_total // HK, axis=1
    ).reshape(local_tokens, lane_total * DH)
    value_flat = mixer_value.reshape(local_tokens, VALUE_HEADS * DH)
    decay_flat = jnp.repeat(
        log_decay.reshape(local_tokens, VALUE_HEADS), lane_total // VALUE_HEADS, axis=1
    )
    strength_flat = jnp.repeat(
        strength.reshape(local_tokens, VALUE_HEADS), lane_total // VALUE_HEADS, axis=1
    )
    received = (
        lax.all_to_all(query_flat, "seq", split_axis=1, concat_axis=0, tiled=True),
        lax.all_to_all(key_flat, "seq", split_axis=1, concat_axis=0, tiled=True),
        lax.all_to_all(value_flat, "seq", split_axis=1, concat_axis=0, tiled=True),
        lax.all_to_all(decay_flat, "seq", split_axis=1, concat_axis=0, tiled=True),
        lax.all_to_all(strength_flat, "seq", split_axis=1, concat_axis=0, tiled=True),
    )
    segment_length = received[0].shape[0]
    block_count = segment_length // BLOCK

    def lanes_first(matrix, width):
        return jnp.transpose(matrix.reshape(block_count, BLOCK, lane_count, width), (2, 0, 1, 3))

    query_lanes = unit_rows(lanes_first(received[0], DH))
    key_lanes = unit_rows(lanes_first(received[1], DH))
    value_lanes = lanes_first(received[2], lane_width).astype(jnp.float32)
    decay_lanes = jnp.transpose(
        received[3].reshape(block_count, BLOCK, lane_count), (2, 0, 1)
    ).astype(jnp.float32)
    strength_lanes = jnp.transpose(
        received[4].reshape(block_count, BLOCK, lane_count), (2, 0, 1)
    ).astype(jnp.float32)
    query_part, local_out, transition, inserted_signal = jax.vmap(block_parts)(
        query_lanes, key_lanes, value_lanes, decay_lanes, strength_lanes
    )
    transition_steps = jnp.moveaxis(transition, 1, 0)
    injection_steps = jnp.moveaxis(inserted_signal, 1, 0)

    def compose(carried, pieces):
        return (
            (apply_map(pieces[0], carried[0]), apply_map(pieces[0], carried[1]) + pieces[1]),
            None,
        )

    identity_lanes = jnp.broadcast_to(jnp.eye(DH, dtype=jnp.float32), (lane_count, DH, DH))
    empty_state = jnp.zeros((lane_count, DH, lane_width), jnp.float32)
    segment_map, unused = lax.scan(
        compose, (identity_lanes, empty_state), (transition_steps, injection_steps)
    )
    all_whole, all_offset = (
        lax.all_gather(segment_map[0][None].astype(jnp.bfloat16), "exp", axis=0, tiled=True).astype(
            jnp.float32
        ),
        lax.all_gather(segment_map[1][None].astype(jnp.bfloat16), "exp", axis=0, tiled=True).astype(
            jnp.float32
        ),
    )
    position = lax.axis_index("exp")

    def fold_prior(step_index, carried):
        stepped = apply_map(all_whole[step_index], carried) + all_offset[step_index]
        return jnp.where(step_index < position, stepped, carried)

    entering = lax.fori_loop(0, exp_devices, fold_prior, empty_state)

    def advance(carried, pieces):
        return (apply_map(pieces[0], carried) + pieces[1], carried)

    final_state, entry_states = lax.scan(advance, entering, (transition_steps, injection_steps))
    head_out = (
        jnp.einsum("lnck,nlkv->lncv", query_part, entry_states, precision=lax.Precision.HIGHEST)
        + local_out
    )
    head_tokens = (
        jnp.transpose(head_out, (1, 2, 0, 3))
        .reshape(segment_length, lane_count * lane_width)
        .astype(jnp.bfloat16)
    )
    head_round = lax.all_to_all(head_tokens, "seq", split_axis=0, concat_axis=1, tiled=True)
    heads_wide = head_round.astype(jnp.float32).reshape(local_tokens, VALUE_HEADS, DH)
    normed = (
        heads_wide
        * lax.rsqrt(jnp.mean(heads_wide * heads_wide, axis=-1, keepdims=True) + 1e-06)
        * out_gain
    )
    mixed = (
        residual.reshape(local_tokens, D).astype(jnp.float32) + normed.reshape(local_tokens, D)
    ).astype(jnp.bfloat16)
    mixed_wide = lax.optimization_barrier(mixed).astype(jnp.float32)
    ffn_in = (
        mixed_wide
        * lax.rsqrt(jnp.mean(mixed_wide * mixed_wide, axis=-1, keepdims=True) + 1e-06)
        * ffn_gain
    ).astype(jnp.bfloat16)
    experts_total = seq_devices * exp_devices
    capacity = max(2, (local_tokens * TOPK + experts_total - 1) // experts_total)
    assign_count = local_tokens * TOPK
    flat_ids = expert_ids.reshape(assign_count)
    sort_order = jnp.argsort(flat_ids, stable=True)
    sorted_ids = flat_ids[sort_order]
    first_seen = jnp.searchsorted(sorted_ids, sorted_ids, side="left")
    sorted_rank = jnp.arange(assign_count, dtype=jnp.int32) - first_seen
    run_rank = jnp.zeros((assign_count,), jnp.int32).at[sort_order].set(sorted_rank)
    slot_index = flat_ids * capacity + run_rank
    token_of = jnp.arange(assign_count, dtype=jnp.int32) // TOPK
    outgoing = (
        jnp.zeros((experts_total * capacity, D), jnp.bfloat16).at[slot_index].set(ffn_in[token_of])
    )
    outgoing = outgoing.reshape(seq_devices, exp_devices, capacity, D)
    arrived = lax.all_to_all(
        lax.all_to_all(outgoing, "seq", split_axis=0, concat_axis=0, tiled=True),
        "exp",
        split_axis=1,
        concat_axis=1,
        tiled=True,
    )
    row_block = arrived.reshape(-1, D)
    gate_value = jnp.dot(row_block, gate_proj[0], preferred_element_type=jnp.float32)
    up_value = jnp.dot(row_block, up_proj[0], preferred_element_type=jnp.float32)
    hidden = (jax.nn.silu(gate_value) * up_value).astype(jnp.bfloat16)
    result = jnp.dot(hidden, down_proj[0], preferred_element_type=jnp.float32).astype(jnp.bfloat16)
    returned = lax.all_to_all(
        lax.all_to_all(
            result.reshape(arrived.shape), "seq", split_axis=0, concat_axis=0, tiled=True
        ),
        "exp",
        split_axis=1,
        concat_axis=1,
        tiled=True,
    )
    per_slot = returned.reshape(experts_total * capacity, D)[slot_index].astype(jnp.float32)
    scaled = per_slot * expert_weights.reshape(assign_count)[:, None]
    ffn_out = jnp.sum(scaled.reshape(local_tokens, TOPK, D), axis=1).astype(jnp.bfloat16)
    return (mixed.reshape(1, local_tokens, D), ffn_out.reshape(1, local_tokens, D))


def solution(mesh):
    return jax.shard_map(
        body,
        mesh=mesh,
        in_specs=(
            P("exp", "seq", None),
            P("exp", "seq", None),
            P("exp", "seq", None),
            P("exp", "seq", None),
            P("exp", "seq", None),
            P("exp", "seq", None),
            P(),
            P(),
            P("exp", "seq", None),
            P("exp", "seq", None),
            P(("seq", "exp"), None, None),
            P(("seq", "exp"), None, None),
            P(("seq", "exp"), None, None),
        ),
        out_specs=(P("exp", "seq", None), P("exp", "seq", None)),
        check_vma=False,
    )
```

profile of v0, /device:TPU:1, one launch (start us, length us, event | category | flops | bytes accessed | tf_op | source)
XLA Modules:
  0.0 874.9 jit_solution(15679718716053557117)
XLA Ops:
  2.0 10.5 %all-to-all-start = ((bf16[64,32,1]{0,2,1:T(2,128)(2,1)}), bf16[64,32,1]{0,2,1:T(2,128)(2,1)S(1)}, u32[]{:S(2)}, u32[]{:S(2)}) async-start(bf16[64,32,1]{0,2,1:T(2,128)(2,1)} %copy.116), calls=%async_computation | async-start | bytes 32768 | tf_op jit(solution)/shard_map/all_to_all | solution.py:108
  13.9 7.3 all-to-all-done
  21.1 3.8 all-to-all-start.3
  25.0 1.5 all_to_all.78
  27.8 5.8 all-to-all-done.3
  33.6 3.9 all-to-all-start.4
  39.3 4.4 sort.17
  43.7 2.8 gather_fusion.1
  48.2 8.5 all-to-all-start.2
  56.7 28.8 %while.66 = (s32[]{:T(128)}, u32[640]{0:T(1024)S(1)}, u32[640]{0:T(1024)S(1)}, s32[640]{0:T(1024)S(1)}, s32[]{:T(128)}, /*index=5*/s32[]{:T(128)}, s32[]{}) while((s32[]{:T(128)}, u32[640]{0:T(1024)S(1)}, u32[640]{0:T(1024)S(1)}, s32[640]{0:T(1024)S(1)}, s32[]{:T(128)}, /*index=5*/s32[]{:T(128)}, s32[]{}) %tuple.124), condition=%wide.region_13.14_spmd.clone, body=%wide.region_12.13_spmd.clone.sunk | while | flops 12548 | bytes 49005 | solution.py:194
  56.7 2.8 gather_fusion
  59.6 2.8 gather_fusion
  62.5 2.8 gather_fusion
  65.4 2.8 gather_fusion
  68.3 2.8 gather_fusion
  71.1 2.8 gather_fusion
  74.0 2.8 gather_fusion
  76.9 2.8 gather_fusion
  79.8 2.8 gather_fusion
  82.7 2.8 gather_fusion
  85.6 4.1 scatter_custom_fusion
  90.8 9.7 %all-to-all-start.1 = ((bf16[64,32,128]{2,0,1:T(8,128)(2,1)}), bf16[64,32,128]{2,0,1:T(8,128)(2,1)S(1)}, u32[]{:S(2)}, u32[]{:S(2)}) async-start(bf16[64,32,128]{2,0,1:T(8,128)(2,1)} %bitcast.16), calls=%async_computation.1 | async-start | bytes 1048576 | tf_op jit(solution)/shard_map/all_to_all | solution.py:105
  101.0 1.2 reshape.636
  102.5 8.9 %all-to-all-done.1 = bf16[64,32,128]{2,0,1:T(8,128)(2,1)S(1)} async-done(((bf16[64,32,128]{2,0,1:T(8,128)(2,1)}), bf16[64,32,128]{2,0,1:T(8,128)(2,1)S(1)}, u32[]{:S(2)}, u32[]{:S(2)}) %all-to-all-start.1) | async-done | bytes 524320 | tf_op jit(solution)/shard_map/all_to_all | solution.py:105
  111.8 2.2 fusion.28
  116.4 1.2 fusion.65
  121.1 1.2 fusion.61
  122.3 1.3 convolution_add_fusion.4
  126.1 1.2 fusion.43
  127.3 1.6 fusion.48
  128.9 3.5 convolution_bitcast_fusion.1
  132.3 5.6 subtract_bitcast_fusion
  137.9 70.2 %while.63 = (s32[]{:T(128)}, f32[1,128,128]{2,1,0:T(8,128)S(1)}, f32[1,128,64]{1,2,0:T(8,128)S(1)}, f32[32,1,128,128]{3,2,1,0:T(8,128)}, f32[32,1,128,64]{2,3,1,0:T(8,128)}, /*index=5*/s32[]{:T(128)}) while((s32[]{:T(128)}, f32[1,128,128]{2,1,0:T(8,128)S(1)}, f32[1,128,64]{1,2,0:T(8,128)S(1)}, f32[32,1,128,128]{3,2,1,0:T(8,128)}, ...), condition=%wide.region_4.5_spmd, body=%wide.region_3.4_spmd.sunk | while | flops 37756928 | bytes 558161 | solution.py:140
  208.1 31.4 %all-gather = bf16[16,128,128]{2,1,0:T(8,128)(2,1)S(1)} all-gather(bf16[1,128,128]{2,1,0:T(8,128)(2,1)S(1)} %convert_element_type.231), channel_id=2, replica_groups=mesh['seq'=32,'exp'=16] {'exp'}, dimensions={0}, use_global_device_ids=true | all-gather | bytes 557056 | tf_op jit(solution)/shard_map/all_gather | solution.py:144
  240.7 15.2 %all-gather.1 = bf16[16,128,64]{1,2,0:T(8,128)(2,1)S(1)} all-gather(bf16[1,128,64]{1,2,0:T(8,128)(2,1)S(1)} %convert_element_type.234), channel_id=3, replica_groups=mesh['seq'=32,'exp'=16] {'exp'}, dimensions={0}, use_global_device_ids=true | all-gather | bytes 278528 | tf_op jit(solution)/shard_map/all_gather | solution.py:147
  256.7 18.1 %while.65 = (s32[]{:T(128)}, f32[1,128,64]{1,2,0:T(8,128)S(1)}, s32[]{:T(128)}, f32[16,1,128,128]{3,2,1,0:T(8,128)}, f32[16,1,128,64]{2,3,1,0:T(8,128)}, /*index=5*/s32[]{:T(128)}, s32[]{:T(128)}) while((s32[]{:T(128)}, f32[1,128,64]{1,2,0:T(8,128)S(1)}, s32[]{:T(128)}, f32[16,1,128,128]{3,2,1,0:T(8,128)}, ...), condition=%wide.region_6.7_spmd.clone, body=%wide.region_5.6_spmd.clone.sunk | while | flops 12615684 | bytes 264807 | solution.py:157
  274.7 55.2 %while.64 = (s32[]{:T(128)}, f32[1,128,64]{1,2,0:T(8,128)S(1)}, f32[32,1,128,64]{2,3,1,0:T(8,128)}, f32[32,1,128,128]{3,2,1,0:T(8,128)}, f32[32,1,128,64]{2,3,1,0:T(8,128)}, /*index=5*/s32[]{:T(128)}) while((s32[]{:T(128)}, f32[1,128,64]{1,2,0:T(8,128)S(1)}, f32[32,1,128,64]{2,3,1,0:T(8,128)}, f32[32,1,128,128]{3,2,1,0:T(8,128)}, ...), condition=%wide.region_8.9_spmd, body=%wide.region_7.8_spmd.sunk | while | flops 12591106 | bytes 296017 | solution.py:162
  330.0 2.2 convolution_multiply_fusion.2
  332.1 2.5 convolution_subtract_fusion
  334.7 1.8 fusion.41
  336.4 1.2 fusion.29
  338.8 5.0 all-to-all-start.5
  343.9 10.0 %all-to-all-done.5 = bf16[32,2,2048]{2,1,0:T(2,128)(2,1)S(1)} async-done(((bf16[32,2,2048]{2,1,0:T(2,128)(2,1)}), bf16[32,2,2048]{2,1,0:T(2,128)(2,1)S(1)}, u32[]{:S(2)}, u32[]{:S(2)}) %all-to-all-start.5) | async-done | bytes 262176 | tf_op jit(solution)/shard_map/all_to_all | solution.py:172
  357.4 23.2 %scatter_custom_fusion.1 = bf16[1024,2048]{1,0:T(8,128)(2,1)} fusion(s32[640]{0:T(1024)S(1)} %compare_select_fusion.1, bf16[64,2048]{1,0:T(8,128)(2,1)S(1)} %fusion.73, s32[1024]{0:T(1024)S(1)} %pad_clamp_fusion.2, bf16[]{:T(256)} %constant.108.clone.1), kind=kCustom, calls=%fused_computation.41 | custom fusion | bytes 4194306 | tf_op jit(solution)/shard_map/scatter | solution.py:200
  380.6 7.8 reshape.552
  388.4 98.9 %all_to_all.95 = bf16[32,16,2,2048]{3,2,1,0:T(2,128)(2,1)S(1)} all-to-all(bf16[32,16,2,2048]{3,2,1,0:T(2,128)(2,1)} %reshape.552), channel_id=1, replica_groups=mesh['seq'=32,'exp'=16] {'seq'}, dimensions={0} | all-to-all | bytes 8388608 | tf_op jit(solution)/shard_map/all_to_all | solution.py:204
  487.3 6.0 copy.134
  493.2 104.3 %all_to_all.96 = bf16[32,16,2,2048]{3,2,0,1:T(2,128)(2,1)S(1)} all-to-all(bf16[32,16,2,2048]{3,2,0,1:T(2,128)(2,1)} %copy.134), channel_id=1, replica_groups=mesh['seq'=32,'exp'=16] {'exp'}, dimensions={1} | all-to-all | bytes 8388608 | tf_op jit(solution)/shard_map/all_to_all | solution.py:203
  597.5 6.5 copy.135
  604.0 7.2 reshape.553
  611.3 4.8 fusion.39
  616.1 9.1 %convolution_convert_fusion = bf16[1024,2048]{1,0:T(8,128)(2,1)} fusion(bf16[1024,2048]{1,0:T(8,128)(2,1)} %reshape.553, bf16[1,256,2048]{2,1,0:T(8,128)(2,1)S(1)} %copy-done, bf16[1,2048,256]{2,1,0:T(8,128)(2,1)} %param.32, f32[1024,256]{1,0:T(8,128)} %fusion.39), kind=kOutput, calls=%fused_computation.40 | convolution fusion | flops 2151153664 | bytes 11534336 | tf_op jit(solution)/shard_map/dot_general | solution.py:214
  625.2 7.6 reshape.554
  632.8 100.5 %all_to_all.97 = bf16[32,16,2,2048]{3,2,1,0:T(2,128)(2,1)S(1)} all-to-all(bf16[32,16,2,2048]{3,2,1,0:T(2,128)(2,1)} %reshape.554), channel_id=1, replica_groups=mesh['seq'=32,'exp'=16] {'seq'}, dimensions={0} | all-to-all | bytes 8388608 | tf_op jit(solution)/shard_map/all_to_all | solution.py:216
  733.3 6.0 copy.136
  739.3 4.6 all-to-all-start.9
  744.0 1.2 reshape.558
  745.3 1.9 fusion.68
  747.2 89.5 %all-to-all-done.9 = bf16[32,16,2,2048]{3,2,0,1:T(2,128)(2,1)} async-done(((bf16[32,16,2,2048]{3,2,0,1:T(2,128)(2,1)}), bf16[32,16,2,2048]{3,2,0,1:T(2,128)(2,1)}, u32[]{:S(2)}, u32[]{:S(2)}) %all-to-all-start.9) | async-done | bytes 4194336 | tf_op jit(solution)/shard_map/all_to_all | solution.py:215
  836.7 8.7 copy.137
  845.4 7.2 reshape.555
  852.6 9.7 %gather_fusion.2 = bf16[640,2048]{1,0:T(8,128)(2,1)} fusion(bf16[1024,2048]{1,0:T(8,128)(2,1)} %reshape.555, s32[1024]{0:T(1024)S(1)} %pad_clamp_fusion.1), kind=kCustom, calls=%fused_computation.3 | custom fusion | bytes 5245440 | tf_op jit(solution)/shard_map/gather | solution.py:224
  862.3 5.8 reshape.561
  868.1 6.6 multiply_reduce_fusion
  (399 shorter events, 165.4 us)
Async XLA Ops:
  0.6 615.4 %copy-start = (bf16[1,256,2048]{2,1,0:T(8,128)(2,1)S(1)}, bf16[1,256,2048]{2,1,0:T(8,128)(2,1)}, u32[]{:S(2)}) copy-start(bf16[1,256,2048]{2,1,0:T(8,128)(2,1)} %param.33) | copy-start | bytes 3145732
  2.0 19.1 %all-to-all-start = ((bf16[64,32,1]{0,2,1:T(2,128)(2,1)}), bf16[64,32,1]{0,2,1:T(2,128)(2,1)S(1)}, u32[]{:S(2)}, u32[]{:S(2)}) async-start(bf16[64,32,1]{0,2,1:T(2,128)(2,1)} %copy.116), calls=%async_computation | async-start | bytes 32768 | tf_op jit(solution)/shard_map/all_to_all | solution.py:108
  21.1 12.4 %all-to-all-start.3 = ((bf16[64,32,1]{0,2,1:T(2,128)(2,1)}), bf16[64,32,1]{0,2,1:T(2,128)(2,1)S(1)}, u32[]{:S(2)}, u32[]{:S(2)}) async-start(bf16[64,32,1]{0,2,1:T(2,128)(2,1)} %copy.119), calls=%async_computation.3 | async-start | bytes 32768 | tf_op jit(solution)/shard_map/all_to_all | solution.py:109
  33.6 13.7 %all-to-all-start.4 = ((bf16[32,2,2048]{2,1,0:T(2,128)(2,1)}), bf16[32,2,2048]{2,1,0:T(2,128)(2,1)S(1)}, u32[]{:S(2)}, u32[]{:S(2)}) async-start(bf16[32,2,2048]{2,1,0:T(2,128)(2,1)} %reshape.635), calls=%async_computation.4 | async-start | bytes 524288 | tf_op jit(solution)/shard_map/all_to_all | solution.py:107
  48.2 41.7 %all-to-all-start.2 = ((bf16[64,32,128]{2,0,1:T(8,128)(2,1)}), bf16[64,32,128]{2,0,1:T(8,128)(2,1)S(1)}, u32[]{:S(2)}, u32[]{:S(2)}) async-start(bf16[64,32,128]{2,0,1:T(8,128)(2,1)} %bitcast.18), calls=%async_computation.2 | async-start | bytes 1048576 | tf_op jit(solution)/shard_map/all_to_all | solution.py:106
  56.7 28.9 %copy-start.7 = (bf16[1,64,1024]{2,1,0:T(8,128)(2,1)S(1)}, bf16[1,64,1024]{2,1,0:T(8,128)(2,1)}, u32[]{:S(2)}) copy-start(bf16[1,64,1024]{2,1,0:T(8,128)(2,1)} %param.21) | copy-start | bytes 393220
  90.8 20.7 %all-to-all-start.1 = ((bf16[64,32,128]{2,0,1:T(8,128)(2,1)}), bf16[64,32,128]{2,0,1:T(8,128)(2,1)S(1)}, u32[]{:S(2)}, u32[]{:S(2)}) async-start(bf16[64,32,128]{2,0,1:T(8,128)(2,1)} %bitcast.16), calls=%async_computation.1 | async-start | bytes 1048576 | tf_op jit(solution)/shard_map/all_to_all | solution.py:105
  122.3 3.7 copy-start.4
  128.9 3.5 copy-start.1
  329.9 4.7 copy-start.5
  334.6 9.2 %copy-start.10 = (f32[128]{0:T(128)S(1)}, f32[128]{0:T(128)}, u32[]{:S(2)}) copy-start(f32[128]{0:T(128)} %param.27) | copy-start | bytes 1540
  337.7 19.2 %copy-start.6 = (bf16[1,64,2048]{2,1,0:T(8,128)(2,1)S(1)}, bf16[1,64,2048]{2,1,0:T(8,128)(2,1)}, u32[]{:S(2)}) copy-start(bf16[1,64,2048]{2,1,0:T(8,128)(2,1)} %param.26) | copy-start | bytes 786436
  338.8 15.1 %all-to-all-start.5 = ((bf16[32,2,2048]{2,1,0:T(2,128)(2,1)}), bf16[32,2,2048]{2,1,0:T(2,128)(2,1)S(1)}, u32[]{:S(2)}, u32[]{:S(2)}) async-start(bf16[32,2,2048]{2,1,0:T(2,128)(2,1)} %reshape.637), calls=%async_computation.5 | async-start | bytes 524288 | tf_op jit(solution)/shard_map/all_to_all | solution.py:172
  354.3 3.0 copy-start.8
  356.1 0.8 copy-start.2
  739.3 4.6 copy-start.9
  739.3 5.9 copy-start.3
  739.3 97.4 %all-to-all-start.9 = ((bf16[32,16,2,2048]{3,2,0,1:T(2,128)(2,1)}), bf16[32,16,2,2048]{3,2,0,1:T(2,128)(2,1)}, u32[]{:S(2)}, u32[]{:S(2)}) async-start(bf16[32,16,2,2048]{3,2,0,1:T(2,128)(2,1)} %copy.136), calls=%async_computation.9 | async-start | bytes 8388608 | tf_op jit(solution)/shard_map/all_to_all | solution.py:215
where the time goes:
time: 887 us; the launch traced here: 875 us
  blocking collectives  350 us (39%)
  matrix products  168 us (19%)
  local copies, waits for them, and re-layouts  166 us (19%)
  waiting for transfers between devices  122 us (14%)
  starting transfers between devices  46 us (5%)
  other arithmetic  17.3 us (2%)
    dot_general x112, matrix products, apply_map(): jnp.einsum('lij,ljk->lik', matrix, carried, precision=lax.Precision.HIGHEST)  120 us
    all_to_all x1, blocking collectives, body(): lax.all_to_all(lax.all_to_all(outgoing, 'seq', split_axis=0, concat_axis=...  104 us
    all_to_all x1, blocking collectives, body(): lax.all_to_all(result.reshape(arrived.shape), 'seq', split_axis=0, concat...  101 us
    all_to_all x1, blocking collectives, body(): lax.all_to_all(outgoing, 'seq', split_axis=0, concat_axis=0, tiled=True)  98.9 us
    all_to_all x1, waiting for transfers between devices, body(): lax.all_to_all(lax.all_to_all(result.reshape(arrived.shape), 'seq', split...  89.5 us
    all_gather x1, blocking collectives, body(): lax.all_gather(segment_map[0][None].astype(jnp.bfloat16), 'exp', axis=0,...  31.4 us
    gather x10, local copies, waits for them, and re-layouts, body(): first_seen = jnp.searchsorted(sorted_ids, sorted_ids, side='left')  27.9 us
    scatter x1, local copies, waits for them, and re-layouts, body(): jnp.zeros((experts_total * capacity, D), jnp.bfloat16).at[slot_index]  23.2 us
  transfers between devices with their start and end apart: 7, of which 6 were waited for; matrix products, arithmetic and copies ran while one was open for 6% of the time, Pallas kernels for 0%

commit v1 on v0

v1 whole, which is shorter than its diff:
```python
import jax
import jax.numpy as jnp
from jax import lax
from jax.experimental import pallas as pl
from jax.experimental.pallas import tpu as pltpu
from jax.sharding import PartitionSpec as P

D = 2048
DH = 128
HK = 8
VALUE_HEADS = 16
TOPK = 10
BLOCK = 64
TOK = 64
EXPERTS = 512
LANES = 32
WIDTH = 64
BLOCKS = 32
CHUNKS = 4
STEPS = 8
SEGMENTS = 16
MAP_ROWS = DH + WIDTH
SLOTS = 2 * EXPERTS
COLS = D // 128
F32 = jnp.float32
BF16 = jnp.bfloat16
VMEM_LIMIT = 56 * 1024 * 1024


def params():
    return pltpu.CompilerParams(vmem_limit_bytes=VMEM_LIMIT)


def full(*arrays):
    return [pl.BlockSpec(memory_space=pltpu.VMEM) for _ in arrays]


def dot_nn(a, b):
    return lax.dot_general(a, b, (((1,), (0,)), ((), ())), preferred_element_type=F32)


def dot_nt(a, b):
    return lax.dot_general(a, b, (((1,), (1,)), ((), ())), preferred_element_type=F32)


def bdot_nn(a, b):
    return lax.dot_general(a, b, (((2,), (1,)), ((0,), (0,))), preferred_element_type=F32)


def bdot_nt(a, b):
    return lax.dot_general(a, b, (((2,), (2,)), ((0,), (0,))), preferred_element_type=F32)


def split(x):
    high = x.astype(BF16)
    return high, (x - high.astype(F32)).astype(BF16)


def bdot3(a, b):
    ah, al = split(a)
    bh, bl = split(b)
    return bdot_nn(ah, bh) + (bdot_nn(ah, bl) + bdot_nn(al, bh))


def swap_matrix():
    out_index = lax.broadcasted_iota(jnp.int32, (256, 256), 0)
    in_index = lax.broadcasted_iota(jnp.int32, (256, 256), 1)
    return (in_index == (out_index % 16) * 16 + out_index // 16).astype(BF16)


def pack_kernel(query_ref, key_ref, value_ref, decay_ref, strength_ref, out_ref):
    lane = lax.broadcasted_iota(jnp.int32, (TOK, 128), 1)
    for index in range(LANES):
        key_head, head, half = index // 4, index // 2, index % 2
        out_ref[index, 0:64, :] = query_ref[:, key_head * 128 : key_head * 128 + 128]
        out_ref[index, 64:128, :] = key_ref[:, key_head * 128 : key_head * 128 + 128]
        piece = value_ref[:, head * 128 : head * 128 + 128].astype(F32)
        if half:
            piece = pltpu.roll(piece, 64, 1)
        decay = jnp.broadcast_to(decay_ref[:, head : head + 1].astype(F32), (TOK, 128))
        strength = jnp.broadcast_to(strength_ref[:, head : head + 1].astype(F32), (TOK, 128))
        piece = jnp.where(lane < 64, piece, jnp.where(lane == 64, decay, strength))
        out_ref[index, 128:192, :] = piece.astype(BF16)


def route_kernel(ids_ref, tok_ref, slot_ref):
    expert = lax.broadcasted_iota(jnp.int32, (TOK, EXPERTS), 1)
    named = jnp.zeros((TOK, EXPERTS), F32)
    for k in range(TOPK):
        named = jnp.where(ids_ref[:, k : k + 1] == expert, 1.0, named)
    row = lax.broadcasted_iota(jnp.int32, (TOK, TOK), 0)
    col = lax.broadcasted_iota(jnp.int32, (TOK, TOK), 1)
    rank = dot_nn((row > col).astype(BF16), named.astype(BF16))
    token = lax.broadcasted_iota(jnp.int32, (TOK, EXPERTS), 0).astype(F32)
    first = jnp.sum(jnp.where(rank == 0.0, token * named, 0.0), axis=0, keepdims=True)
    second = jnp.sum(jnp.where(rank == 1.0, token * named, 0.0), axis=0, keepdims=True)
    tok_ref[...] = jnp.concatenate([first, second], axis=0).astype(jnp.int32)
    lane = lax.broadcasted_iota(jnp.int32, (TOK, 128), 1)
    slots = jnp.zeros((TOK, 128), jnp.int32)
    for k in range(TOPK):
        ids = ids_ref[:, k : k + 1]
        mine = jnp.sum(jnp.where(ids == expert, rank, 0.0), axis=1, keepdims=True)
        slots = jnp.where(lane == k, 2 * ids + mine.astype(jnp.int32), slots)
    slot_ref[...] = slots


def mixer_kernel(
    recv_ref,
    query_part_ref,
    local_ref,
    sub_map_ref,
    sub_gain_ref,
    send_ref,
    w_ref,
    u_ref,
    k_ref,
    gain_ref,
):
    row = lax.broadcasted_iota(jnp.int32, (BLOCK, BLOCK), 0)
    col = lax.broadcasted_iota(jnp.int32, (BLOCK, BLOCK), 1)
    eye = (row == col)[None]
    inclusive = (row >= col)[None]
    upper = (row <= col)[None]
    lower = (row > col)[None]
    group = STEPS

    def same(size):
        return ((row // size) == (col // size))[None]

    identity = jnp.broadcast_to(eye.astype(F32), (group, BLOCK, BLOCK))
    identity_half = identity.astype(BF16)

    def parts(step, unused):
        start = step * group
        block = recv_ref[pl.ds(start, group)]
        q = block[:, 0:64]
        k = block[:, 64:128]
        extra = block[:, 128:192]
        qf = q.astype(F32)
        kf = k.astype(F32)
        q_norm = lax.rsqrt(jnp.sum(qf * qf, axis=2, keepdims=True) + 1e-06)
        k_norm = lax.rsqrt(jnp.sum(kf * kf, axis=2, keepdims=True) + 1e-06)
        k_norm_row = jnp.sum(jnp.where(eye, k_norm, 0.0), axis=1, keepdims=True)
        decay = extra[:, :, 64:65].astype(F32)
        strength = extra[:, :, 65:66].astype(F32)
        strength_row = jnp.sum(jnp.where(eye, strength, 0.0), axis=1, keepdims=True)
        decay_row = jnp.sum(jnp.where(eye, decay, 0.0), axis=1, keepdims=True)
        cum_row = jnp.sum(jnp.where(upper, decay, 0.0), axis=1, keepdims=True)
        cum = jnp.sum(jnp.where(inclusive, decay_row, 0.0), axis=2, keepdims=True)
        spread = cum - cum_row
        fade = jnp.where(inclusive, jnp.exp(jnp.where(inclusive, spread, 0.0)), 0.0)
        key_dot = bdot_nt(k, k) * (k_norm * k_norm_row)
        query_dot = bdot_nt(q, k) * (q_norm * k_norm_row)
        negated = jnp.where(lower, -(strength * key_dot * fade), 0.0)
        base = jnp.where(same(8), negated, 0.0)
        inverse = identity + base
        powered = bdot3(base, base)
        inverse = inverse + bdot3(inverse, powered)
        powered = bdot3(powered, powered)
        inverse = inverse + bdot3(inverse, powered)
        for size in (8, 16, 32):
            cross = jnp.where(same(2 * size) & ~same(size), negated, 0.0).astype(BF16)
            half = inverse.astype(BF16)
            inverse = inverse + bdot_nn(bdot_nn(half, cross).astype(BF16), half)
        inverse_half = inverse.astype(BF16)
        decay_gain = jnp.exp(cum)
        last = cum[:, BLOCK - 1 : BLOCK, :]
        tail = jnp.exp(last - cum)
        unit_k = k_norm * kf
        w = bdot_nn(inverse_half, ((strength * decay_gain) * unit_k).astype(BF16)).astype(BF16)
        v_t = bdot_nt(identity_half, extra[:, :, 0:64]) * strength_row
        u_t = bdot_nt(v_t.astype(BF16), inverse_half)
        scores = (query_dot * fade).astype(BF16)
        q_part = decay_gain * (q_norm * qf) - bdot_nn(scores, w)
        local = bdot_nt(scores, u_t.astype(BF16))
        w_ref[pl.ds(start, group)] = w
        u_ref[pl.ds(start, group)] = u_t
        k_ref[pl.ds(start, group)] = (tail * unit_k).astype(BF16)
        gain_ref[pl.ds(start, group)] = jnp.broadcast_to(jnp.exp(last), (group, 8, 128))
        query_part_ref[pl.ds(start, group)] = q_part.astype(BF16)
        local_ref[pl.ds(start, group)] = local
        return unused

    lax.fori_loop(0, BLOCKS // group, parts, 0)

    map_row = lax.broadcasted_iota(jnp.int32, (MAP_ROWS, DH), 0)
    map_col = lax.broadcasted_iota(jnp.int32, (MAP_ROWS, DH), 1)
    diagonal = map_row == map_col
    start_map = jnp.where(diagonal, 1.0, 0.0).astype(F32)

    def advance(step, carried):
        maps, gains = carried
        new_maps, new_gains = [], []
        for chunk in range(CHUNKS):
            index = chunk * STEPS + step
            state = maps[chunk]
            half = state.astype(BF16)
            out = dot_nt(query_part_ref[index], half)
            seen = dot_nt(half, w_ref[index])
            fresh = jnp.concatenate([-seen[0:DH], u_ref[index] - seen[DH:MAP_ROWS]], axis=0)
            gain = gain_ref[index][0:1, :]
            query_part_ref[index] = out[:, 0:DH].astype(BF16)
            local_ref[index] = local_ref[index] + out[:, DH:MAP_ROWS]
            new_maps.append(gain * state + dot_nn(fresh.astype(BF16), k_ref[index]))
            new_gains.append(gain * gains[chunk])
        return tuple(new_maps), tuple(new_gains)

    maps, gains = lax.fori_loop(
        0,
        STEPS,
        advance,
        (
            tuple(start_map for _ in range(CHUNKS)),
            tuple(jnp.ones((1, DH), F32) for _ in range(CHUNKS)),
        ),
    )
    whole = None
    for chunk in range(CHUNKS):
        gain = gains[chunk]
        changed = maps[chunk] - jnp.where(diagonal, gain, 0.0)
        sub_map_ref[chunk] = changed
        sub_gain_ref[chunk] = jnp.broadcast_to(gain, (8, DH))
        if whole is None:
            whole, total = maps[chunk], gain
        else:
            added = jnp.where(map_row < DH, 0.0, changed)
            whole = gain * whole + dot_nn(whole.astype(BF16), changed[0:DH].astype(BF16)) + added
            total = gain * total
    send_ref[0:MAP_ROWS, :] = (whole - jnp.where(diagonal, total, 0.0)).astype(BF16)
    high, low = split(total)
    send_ref[MAP_ROWS : MAP_ROWS + 16, :] = jnp.broadcast_to(high.astype(F32), (16, DH)).astype(BF16)
    send_ref[MAP_ROWS + 16 : MAP_ROWS + 32, :] = jnp.broadcast_to(low.astype(F32), (16, DH)).astype(BF16)


def fold_kernel(
    position_ref, maps_ref, query_part_ref, local_ref, sub_map_ref, sub_gain_ref, out_ref
):
    def fold(index, state):
        gain = (
            maps_ref[index, MAP_ROWS : MAP_ROWS + 16, :].astype(F32)
            + maps_ref[index, MAP_ROWS + 16 : MAP_ROWS + 32, :].astype(F32)
        )[0:1]
        return (
            gain * state
            + dot_nn(state.astype(BF16), maps_ref[index, 0:DH, :])
            + maps_ref[index, DH:MAP_ROWS, :].astype(F32)
        )

    state = lax.fori_loop(0, position_ref[0], fold, jnp.zeros((WIDTH, DH), F32))
    for chunk in range(CHUNKS):
        half = state.astype(BF16)
        for step in range(STEPS):
            index = chunk * STEPS + step
            out = dot_nt(query_part_ref[index], half) + local_ref[index]
            out_ref[index] = jnp.concatenate([out[0:32], out[32:64]], axis=1).astype(BF16)
        if chunk + 1 < CHUNKS:
            changed = sub_map_ref[chunk]
            state = (
                sub_gain_ref[chunk][0:1] * state
                + dot_nn(half, changed[0:DH].astype(BF16))
                + changed[DH:MAP_ROWS]
            )


def mixed_kernel(
    tok_ref, heads_ref, residual_ref, out_gain_ref, ffn_gain_ref, mixed_ref, send_ref, rows_ref
):
    lane = lax.broadcasted_iota(jnp.int32, (32, 128), 1)
    gain = out_gain_ref[...]
    total = jnp.zeros((TOK, 1), F32)
    for head in range(VALUE_HEADS):
        left = heads_ref[2 * head].astype(F32)
        right = heads_ref[2 * head + 1].astype(F32)
        top = jnp.where(lane < 64, left, pltpu.roll(right, 64, 1))
        bottom = jnp.where(lane < 64, pltpu.roll(left, 64, 1), right)
        wide = jnp.concatenate([top, bottom], axis=0)
        scale = lax.rsqrt(jnp.mean(wide * wide, axis=1, keepdims=True) + 1e-06)
        part = slice(head * DH, head * DH + DH)
        mixed = (residual_ref[:, part].astype(F32) + wide * scale * gain).astype(BF16)
        mixed_ref[:, part] = mixed
        mixed_wide = mixed.astype(F32)
        total = total + jnp.sum(mixed_wide * mixed_wide, axis=1, keepdims=True)
    scale = lax.rsqrt(total * (1.0 / D) + 1e-06)
    swap = swap_matrix()
    for group in range(TOK // 16):
        tokens = slice(group * 16, group * 16 + 16)
        pieces = []
        for c in range(COLS):
            part = slice(c * 128, c * 128 + 128)
            value = mixed_ref[tokens, part].astype(F32) * scale[tokens] * ffn_gain_ref[:, part]
            pieces.append(value.astype(BF16))
        swapped = dot_nn(swap, jnp.concatenate(pieces, axis=0)).astype(BF16)
        rows_ref[tokens] = swapped.reshape(16, 16, 128)

    def place(expert, unused):
        send_ref[2 * expert] = rows_ref[tok_ref[0, expert]]
        send_ref[2 * expert + 1] = rows_ref[tok_ref[1, expert]]
        return unused

    lax.fori_loop(0, EXPERTS, place, 0, unroll=16)


FFN_ROWS = 256


def expert_kernel(rows_ref, gate_ref, up_ref, down_ref, out_ref, wide_ref):
    swap = swap_matrix()
    for group in range(FFN_ROWS // 16):
        tile = dot_nn(swap, rows_ref[group * 256 : group * 256 + 256, :]).astype(BF16)
        for c in range(COLS):
            wide_ref[group * 16 : group * 16 + 16, c * 128 : c * 128 + 128] = tile[
                c * 16 : c * 16 + 16
            ]
    wide = wide_ref[...]
    gate = dot_nn(wide, gate_ref[...])
    up = dot_nn(wide, up_ref[...])
    hidden = (gate / (1.0 + jnp.exp(-gate)) * up).astype(BF16)
    wide_ref[...] = dot_nn(hidden, down_ref[...]).astype(BF16)
    for group in range(FFN_ROWS // 16):
        pieces = [
            wide_ref[group * 16 : group * 16 + 16, c * 128 : c * 128 + 128] for c in range(COLS)
        ]
        out_ref[group * 256 : group * 256 + 256, :] = dot_nn(
            swap, jnp.concatenate(pieces, axis=0)
        ).astype(BF16)


def combine_kernel(slot_ref, weight_ref, rows_ref, out_ref, sum_ref):
    def token(index, unused):
        total = jnp.zeros((16, 128), F32)
        for k in range(TOPK):
            total = total + weight_ref[index, k] * rows_ref[slot_ref[index, k]].astype(F32)
        sum_ref[index] = total.astype(BF16)
        return unused

    lax.fori_loop(0, TOK, token, 0, unroll=2)
    swap = swap_matrix()
    for group in range(TOK // 16):
        tokens = slice(group * 16, group * 16 + 16)
        tile = dot_nn(swap, sum_ref[tokens].reshape(256, 128)).astype(BF16)
        for c in range(COLS):
            out_ref[tokens, c * 128 : c * 128 + 128] = tile[c * 16 : c * 16 + 16]


def shape(dims, dtype):
    return jax.ShapeDtypeStruct(dims, dtype)


SMEM = pl.BlockSpec(memory_space=pltpu.SMEM)
WHOLE = pl.BlockSpec(memory_space=pltpu.VMEM)


def pack(query, key, value, decay, strength):
    return pl.pallas_call(
        pack_kernel,
        out_shape=shape((LANES, 192, 128), BF16),
        in_specs=[WHOLE] * 5,
        out_specs=WHOLE,
        compiler_params=params(),
        name="pack",
    )(query, key, value, decay, strength)


def route(ids):
    return pl.pallas_call(
        route_kernel,
        out_shape=(shape((2, EXPERTS), jnp.int32), shape((TOK, 128), jnp.int32)),
        in_specs=[WHOLE],
        out_specs=(WHOLE, WHOLE),
        compiler_params=params(),
        name="route",
    )(ids)


def mixer(received):
    return pl.pallas_call(
        mixer_kernel,
        out_shape=(
            shape((BLOCKS, BLOCK, DH), BF16),
            shape((BLOCKS, BLOCK, WIDTH), F32),
            shape((CHUNKS, MAP_ROWS, DH), F32),
            shape((CHUNKS, 8, DH), F32),
            shape((MAP_ROWS + 32, DH), BF16),
        ),
        in_specs=[WHOLE],
        out_specs=(WHOLE,) * 5,
        scratch_shapes=[
            pltpu.VMEM((BLOCKS, BLOCK, DH), BF16),
            pltpu.VMEM((BLOCKS, WIDTH, BLOCK), F32),
            pltpu.VMEM((BLOCKS, BLOCK, DH), BF16),
            pltpu.VMEM((BLOCKS, 8, DH), F32),
        ],
        compiler_params=params(),
        name="mixer",
    )(received)


def fold(position, maps, query_part, local, sub_map, sub_gain):
    return pl.pallas_call(
        fold_kernel,
        out_shape=shape((BLOCKS, 32, 128), BF16),
        in_specs=[SMEM] + [WHOLE] * 5,
        out_specs=WHOLE,
        compiler_params=params(),
        name="fold",
    )(position, maps, query_part, local, sub_map, sub_gain)


def mix(tok, heads, residual, out_gain, ffn_gain):
    return pl.pallas_call(
        mixed_kernel,
        out_shape=(shape((TOK, D), BF16), shape((SLOTS, 16, 128), BF16)),
        in_specs=[SMEM] + [WHOLE] * 4,
        out_specs=(WHOLE, WHOLE),
        scratch_shapes=[pltpu.VMEM((TOK, 16, 128), BF16)],
        compiler_params=params(),
        name="mix",
    )(tok, heads, residual, out_gain, ffn_gain)


def experts(rows, gate, up, down):
    hidden = gate.shape[1]
    block = pl.BlockSpec((FFN_ROWS * 16, 128), lambda i: (i, 0))
    return pl.pallas_call(
        expert_kernel,
        grid=(SLOTS // FFN_ROWS,),
        out_shape=shape((SLOTS * 16, 128), BF16),
        in_specs=[
            block,
            pl.BlockSpec((D, hidden), lambda i: (0, 0)),
            pl.BlockSpec((D, hidden), lambda i: (0, 0)),
            pl.BlockSpec((hidden, D), lambda i: (0, 0)),
        ],
        out_specs=block,
        scratch_shapes=[pltpu.VMEM((FFN_ROWS, D), BF16)],
        compiler_params=params(),
        name="experts",
    )(rows, gate, up, down)


def combine(slots, weights, rows):
    return pl.pallas_call(
        combine_kernel,
        out_shape=shape((TOK, D), BF16),
        in_specs=[SMEM, SMEM, WHOLE],
        out_specs=WHOLE,
        scratch_shapes=[pltpu.VMEM((TOK, 16, 128), BF16)],
        compiler_params=params(),
        name="combine",
    )(slots, weights, rows)


def swap_all(x, axes):
    return lax.all_to_all(x, axes, split_axis=0, concat_axis=0, tiled=True)


def body(
    mixer_query,
    mixer_key,
    mixer_value,
    log_decay,
    strength,
    residual,
    out_gain,
    ffn_gain,
    expert_ids,
    expert_weights,
    gate_proj,
    up_proj,
    down_proj,
):
    sent = pack(mixer_query[0], mixer_key[0], mixer_value[0], log_decay[0], strength[0])
    received = swap_all(sent, "seq")
    tok, slots = route(expert_ids[0])
    query_part, local, sub_map, sub_gain, own_map = mixer(received)
    maps = lax.all_gather(own_map, "exp", axis=0)
    position = lax.axis_index("exp").astype(jnp.int32).reshape(1)
    head_rows = fold(position, maps, query_part, local, sub_map, sub_gain)
    heads = swap_all(head_rows, "seq")
    mixed, outgoing = mix(
        tok, heads, residual[0], out_gain.reshape(1, DH), ffn_gain.reshape(1, D)
    )
    arrived = swap_all(outgoing, ("seq", "exp"))
    result = experts(arrived.reshape(SLOTS * 16, 128), gate_proj[0], up_proj[0], down_proj[0])
    returned = swap_all(result.reshape(SLOTS, 16, 128), ("seq", "exp"))
    ffn_out = combine(slots, expert_weights[0], returned)
    return (mixed[None], ffn_out[None])


def solution(mesh):
    rows = P("exp", "seq", None)
    owned = P(("seq", "exp"), None, None)
    return jax.shard_map(
        body,
        mesh=mesh,
        in_specs=(rows,) * 6 + (P(), P(), rows, rows) + (owned,) * 3,
        out_specs=(rows, rows),
        check_vma=False,
    )
```

time: 887 us -> 366 us (0.41); the launches traced: 875 us -> 366 us
  blocking collectives: 350 us -> 141 us
  matrix products: 168 us -> 0 us
  local copies, waits for them, and re-layouts: 166 us -> 6.04 us
  Pallas kernels: 0 us -> 50.2 us
  starting transfers between devices: 46 us -> 28.6 us
  other arithmetic: 17.3 us -> 0 us
  waiting for transfers between devices: 122 us -> 139 us
    all_to_all x3 -> x1, blocking collectives: 304 us -> 111 us  [swap_all(): return lax.all_to_all(x, axes, split_axis=0, concat_axis=0, tiled=True)]
    dot_general x133 -> x0, matrix products: 168 us -> none  [the longest x112 120 us: apply_map(): jnp.einsum('lij,ljk->lik', matrix, carried, precision=lax.Precision.HIGHEST)]
    pallas_call x0 -> x7, Pallas kernels: none -> 50.2 us  [the longest x1 17.9 us: mixer(): pl.pallas_call(mixer_kernel, out_shape=(shape((BLOCKS, BLOCK, DH), BF16),...]
    gather x12 -> x0, local copies, waits for them, and re-layouts: 40.4 us -> none  [the longest x10 27.9 us: body(): first_seen = jnp.searchsorted(sorted_ids, sorted_ids, side='left')]
    all_to_all x8 -> x0, local copies, waits for them, and re-layouts: 30.1 us -> none  [the longest x1 8.69 us: body(): lax.all_to_all(lax.all_to_all(result.reshape(arrived.shape), 'seq', split...]
    reshape x7 -> x0, local copies, waits for them, and re-layouts: 30 us -> none  [the longest x1 7.78 us: body(): outgoing = outgoing.reshape(seq_devices, exp_devices, capacity, D)]
    scatter x2 -> x0, local copies, waits for them, and re-layouts: 27.3 us -> none  [the longest x1 23.2 us: body(): jnp.zeros((experts_total * capacity, D), jnp.bfloat16).at[slot_index]]
    dynamic_update_slice x32 -> x0, local copies, waits for them, and re-layouts: 19.5 us -> none  [body(): lax.scan(advance, entering, (transition_steps, injection_steps))]
  transfers between devices with their start and end apart: 7 -> 3, of which waited for: 6 -> 3; matrix products, arithmetic and copies ran while one was open for 6% -> 0% of each run, Pallas kernels for 0% -> 1%
where the time goes in v1:
time: 366 us
  blocking collectives  141 us (39%)
  waiting for transfers between devices  139 us (38%)
  Pallas kernels  50.2 us (14%)
  starting transfers between devices  28.6 us (8%)
  local copies, waits for them, and re-layouts  6.04 us (2%)
    all_to_all x3, waiting for transfers between devices, swap_all(): return lax.all_to_all(x, axes, split_axis=0, concat_axis=0, tiled=True)  139 us
    all_to_all x1, blocking collectives, swap_all(): return lax.all_to_all(x, axes, split_axis=0, concat_axis=0, tiled=True)  111 us
    all_gather x1, blocking collectives, body(): maps = lax.all_gather(own_map, 'exp', axis=0)  30.5 us
    all_to_all x3, starting transfers between devices, swap_all(): return lax.all_to_all(x, axes, split_axis=0, concat_axis=0, tiled=True)  28.6 us
    pallas_call x1, Pallas kernels, mixer(): pl.pallas_call(mixer_kernel, out_shape=(shape((BLOCKS, BLOCK, DH), BF16),...  17.9 us
    pallas_call x1, Pallas kernels, experts(): pl.pallas_call(expert_kernel, grid=(SLOTS // FFN_ROWS,), out_shape=shape(...  12.3 us
  transfers between devices with their start and end apart: 3, of which 3 were waited for; matrix products, arithmetic and copies ran while one was open for 0% of the time, Pallas kernels for 1%

profile of v1, /device:TPU:1, one launch (start us, length us, event | category | flops | bytes accessed | tf_op | source)
XLA Modules:
  0.0 365.6 jit_solution(14781987099634424234)
XLA Ops:
  0.6 1.4 copy.16
  2.0 1.4 copy.17
  3.4 2.8 pack.1
  6.2 0.0 copy-start.2
  6.2 10.6 %all-to-all-start = ((bf16[32,192,128]{2,1,0:T(8,128)(2,1)}), bf16[32,192,128]{2,1,0:T(8,128)(2,1)S(1)}, u32[]{:S(2)}, u32[]{:S(2)}) async-start(bf16[32,192,128]{2,1,0:T(8,128)(2,1)} %pack.1), calls=%async_computation | async-start | bytes 3145728 | tf_op jit(solution)/shard_map/all_to_all | solution.py:454
  16.8 36.9 %all-to-all-done.recv_ref = bf16[32,192,128]{2,1,0:T(8,128)(2,1)S(1)} async-done(((bf16[32,192,128]{2,1,0:T(8,128)(2,1)}), bf16[32,192,128]{2,1,0:T(8,128)(2,1)S(1)}, u32[]{:S(2)}, u32[]{:S(2)}) %all-to-all-start) | async-done | bytes 1572896 | tf_op jit(solution)/shard_map/all_to_all | solution.py:454
  53.7 0.0 copy-start
  53.7 1.2 copy-done
  54.9 17.9 %mixer.1 = (bf16[32,64,128]{2,1,0:T(8,128)(2,1)}, f32[32,64,64]{2,1,0:T(8,128)}, f32[4,192,128]{2,1,0:T(8,128)}, f32[4,8,128]{2,1,0:T(8,128)}, bf16[224,128]{1,0:T(8,128)(2,1)}) custom-call(bf16[32,192,128]{2,1,0:T(8,128)(2,1)} %copy-done), custom_call_target="tpu_custom_call" | custom-call | tf_op jit(solution)/shard_map/mixer/pallas_call | solution.py:376
  72.8 30.5 %all-gather = bf16[3584,128]{1,0:T(8,128)(2,1)} all-gather(bf16[224,128]{1,0:T(8,128)(2,1)} %get-tuple-element.12), channel_id=2, replica_groups=mesh['seq'=32,'exp'=16] {'exp'}, dimensions={0}, use_global_device_ids=true | all-gather | bytes 974848 | tf_op jit(solution)/shard_map/all_gather | solution.py:476
  103.3 3.5 fold.1
  106.9 5.3 %all-to-all-start.1 = ((bf16[32,32,128]{2,1,0:T(8,128)(2,1)}), bf16[32,32,128]{2,1,0:T(8,128)(2,1)S(1)}, u32[]{:S(2)}, u32[]{:S(2)}) async-start(bf16[32,32,128]{2,1,0:T(8,128)(2,1)} %fold.1), calls=%async_computation.1 | async-start | bytes 524288 | tf_op jit(solution)/shard_map/all_to_all | solution.py:454
  112.3 0.0 copy-done.2
  112.3 0.7 copy.15
  113.0 3.1 route.1
  116.1 6.5 %all-to-all-done.1.heads_ref = bf16[32,32,128]{2,1,0:T(8,128)(2,1)S(1)} async-done(((bf16[32,32,128]{2,1,0:T(8,128)(2,1)}), bf16[32,32,128]{2,1,0:T(8,128)(2,1)S(1)}, u32[]{:S(2)}, u32[]{:S(2)}) %all-to-all-start.1) | async-done | bytes 262176 | tf_op jit(solution)/shard_map/all_to_all | solution.py:454
  122.5 0.0 copy-start.1
  122.5 0.7 copy-done.1
  123.2 6.3 %mix.1 = (bf16[64,2048]{1,0:T(8,128)(2,1)}, bf16[1024,16,128]{2,1,0:T(8,128)(2,1)}) custom-call(s32[2,512]{1,0:T(2,128)} %get-tuple-element.11.tok_ref, bf16[32,32,128]{2,1,0:T(8,128)(2,1)} %copy-done.1, bf16[64,2048]{1,0:T(8,128)(2,1)} %bitcast.26, f32[1,128]{1,0:T(1,128)} %bitcast.35, f32[1,2048]{1,0:T(1,128)} %bitcast.34), custom_call_target="tpu_custom_call" | custom-call | tf_op jit(solution)/shard_map/mix/pallas_call | solution.py:410
  129.5 110.9 %all_to_all.20 = bf16[1024,16,128]{2,1,0:T(8,128)(2,1)} all-to-all(bf16[1024,16,128]{2,1,0:T(8,128)(2,1)} %get-tuple-element.19), channel_id=1, replica_groups=mesh['seq'=32,'exp'=16] {'seq','exp'}, dimensions={0} | all-to-all | bytes 8388608 | tf_op jit(solution)/shard_map/all_to_all | solution.py:454
  240.4 12.3 %experts.1 = bf16[16384,128]{1,0:T(8,128)(2,1)} custom-call(bf16[16384,128]{1,0:T(8,128)(2,1)} %bitcast.20, bf16[2048,256]{1,0:T(8,128)(2,1)} %bitcast.22, bf16[2048,256]{1,0:T(8,128)(2,1)} %bitcast.23, bf16[256,2048]{1,0:T(8,128)(2,1)} %bitcast.24), custom_call_target="tpu_custom_call" | custom-call | tf_op jit(solution)/shard_map/experts/pallas_call | solution.py:424
  252.6 0.0 copy-start.3
  252.6 12.6 %all-to-all-start.3 = ((bf16[1024,16,128]{2,1,0:T(8,128)(2,1)}), bf16[1024,16,128]{2,1,0:T(8,128)(2,1)}, u32[]{:S(2)}, u32[]{:S(2)}) async-start(bf16[1024,16,128]{2,1,0:T(8,128)(2,1)} %bitcast.19), calls=%async_computation.3 | async-start | bytes 8388608 | tf_op jit(solution)/shard_map/all_to_all | solution.py:454
  265.2 0.0 copy-done.3
  265.3 0.7 copy.18
  266.0 95.4 %all-to-all-done.3.rows_ref = bf16[1024,16,128]{2,1,0:T(8,128)(2,1)} async-done(((bf16[1024,16,128]{2,1,0:T(8,128)(2,1)}), bf16[1024,16,128]{2,1,0:T(8,128)(2,1)}, u32[]{:S(2)}, u32[]{:S(2)}) %all-to-all-start.3) | async-done | bytes 4194336 | tf_op jit(solution)/shard_map/all_to_all | solution.py:454
  361.3 4.3 %combine.1 = bf16[64,2048]{1,0:T(8,128)(2,1)} custom-call(s32[64,128]{1,0:T(8,128)} %get-tuple-element.18.slot_ref, f32[64,10]{1,0:T(8,128)} %bitcast.28, bf16[1024,16,128]{2,1,0:T(8,128)(2,1)} %all-to-all-done.3.rows_ref), custom_call_target="tpu_custom_call" | custom-call | tf_op jit(solution)/shard_map/combine/pallas_call | solution.py:442
Async XLA Ops:
  6.2 106.1 %copy-start.2 = (s32[1,64,10]{1,0,2:T(1,128)S(1)}, s32[1,64,10]{1,0,2:T(1,128)}, u32[]{:S(2)}) copy-start(s32[1,64,10]{1,0,2:T(1,128)} %param.21) | copy-start | bytes 7684
  6.2 47.5 %all-to-all-start = ((bf16[32,192,128]{2,1,0:T(8,128)(2,1)}), bf16[32,192,128]{2,1,0:T(8,128)(2,1)S(1)}, u32[]{:S(2)}, u32[]{:S(2)}) async-start(bf16[32,192,128]{2,1,0:T(8,128)(2,1)} %pack.1), calls=%async_computation | async-start | bytes 3145728 | tf_op jit(solution)/shard_map/all_to_all | solution.py:454
  53.7 1.2 copy-start
  106.9 15.6 %all-to-all-start.1 = ((bf16[32,32,128]{2,1,0:T(8,128)(2,1)}), bf16[32,32,128]{2,1,0:T(8,128)(2,1)S(1)}, u32[]{:S(2)}, u32[]{:S(2)}) async-start(bf16[32,32,128]{2,1,0:T(8,128)(2,1)} %fold.1), calls=%async_computation.1 | async-start | bytes 524288 | tf_op jit(solution)/shard_map/all_to_all | solution.py:454
  122.5 0.7 copy-start.1
  252.6 12.6 %copy-start.3 = (f32[1,64,10]{1,0,2:T(1,128)S(1)}, f32[1,64,10]{1,0,2:T(1,128)}, u32[]{:S(2)}) copy-start(f32[1,64,10]{1,0,2:T(1,128)} %param.22) | copy-start | bytes 7684
  252.6 108.7 %all-to-all-start.3 = ((bf16[1024,16,128]{2,1,0:T(8,128)(2,1)}), bf16[1024,16,128]{2,1,0:T(8,128)(2,1)}, u32[]{:S(2)}, u32[]{:S(2)}) async-start(bf16[1024,16,128]{2,1,0:T(8,128)(2,1)} %bitcast.19), calls=%async_computation.3 | async-start | bytes 8388608 | tf_op jit(solution)/shard_map/all_to_all | solution.py:454

commit v2 on v1

--- a/solution.py
+++ b/solution.py
@@ -3,6 +3,7 @@
 from jax import lax
 from jax.experimental import pallas as pl
 from jax.experimental.pallas import tpu as pltpu
+from jax.sharding import Mesh
 from jax.sharding import PartitionSpec as P
 
 D = 2048
@@ -13,18 +14,20 @@
 BLOCK = 64
 TOK = 64
 EXPERTS = 512
-LANES = 32
 WIDTH = 64
-BLOCKS = 32
+BLOCKS = 16
+GROUP = 8
 CHUNKS = 4
-STEPS = 8
-SEGMENTS = 16
-MAP_ROWS = DH + WIDTH
+STEPS = 4
+PACK_ROWS = 3 * TOK + 16
+MAP_ROWS = 2 * DH
+HALF_ROWS = MAP_ROWS + 32
+SEG_ROWS = DH + WIDTH + 32
 SLOTS = 2 * EXPERTS
 COLS = D // 128
 F32 = jnp.float32
 BF16 = jnp.bfloat16
-VMEM_LIMIT = 56 * 1024 * 1024
+VMEM_LIMIT = 28 * 1024 * 1024
 
 
 def params():
@@ -69,21 +72,16 @@
 
 
 def pack_kernel(query_ref, key_ref, value_ref, decay_ref, strength_ref, out_ref):
-    lane = lax.broadcasted_iota(jnp.int32, (TOK, 128), 1)
-    for index in range(LANES):
-        key_head, head, half = index // 4, index // 2, index % 2
-        out_ref[index, 0:64, :] = query_ref[:, key_head * 128 : key_head * 128 + 128]
-        out_ref[index, 64:128, :] = key_ref[:, key_head * 128 : key_head * 128 + 128]
-        piece = value_ref[:, head * 128 : head * 128 + 128].astype(F32)
-        if half:
-            piece = pltpu.roll(piece, 64, 1)
-        decay = jnp.broadcast_to(decay_ref[:, head : head + 1].astype(F32), (TOK, 128))
-        strength = jnp.broadcast_to(strength_ref[:, head : head + 1].astype(F32), (TOK, 128))
-        piece = jnp.where(lane < 64, piece, jnp.where(lane == 64, decay, strength))
-        out_ref[index, 128:192, :] = piece.astype(BF16)
-
-
-def route_kernel(ids_ref, tok_ref, slot_ref):
+    gates = jnp.concatenate([decay_ref[...].astype(F32), strength_ref[...].astype(F32)], axis=1)
+    for head in range(VALUE_HEADS):
+        shared = slice(head // 2 * DH, head // 2 * DH + DH)
+        out_ref[head, 0:64, :] = query_ref[:, shared]
+        out_ref[head, 64:128, :] = key_ref[:, shared]
+        out_ref[head, 128:192, :] = value_ref[:, head * DH : head * DH + DH]
+        out_ref[head, 192:208, :] = jnp.broadcast_to(gates[head : head + 1], (16, 128)).astype(BF16)
+
+
+def route_kernel(ids_ref, weight_in_ref, tok_ref, slot_ref, weight_ref):
     expert = lax.broadcasted_iota(jnp.int32, (TOK, EXPERTS), 1)
     named = jnp.zeros((TOK, EXPERTS), F32)
     for k in range(TOPK):
@@ -97,11 +95,27 @@
     tok_ref[...] = jnp.concatenate([first, second], axis=0).astype(jnp.int32)
     lane = lax.broadcasted_iota(jnp.int32, (TOK, 128), 1)
     slots = jnp.zeros((TOK, 128), jnp.int32)
+    weights = jnp.zeros((TOK, 128), F32)
     for k in range(TOPK):
         ids = ids_ref[:, k : k + 1]
         mine = jnp.sum(jnp.where(ids == expert, rank, 0.0), axis=1, keepdims=True)
         slots = jnp.where(lane == k, 2 * ids + mine.astype(jnp.int32), slots)
+        weights = jnp.where(lane == k, weight_in_ref[:, k : k + 1], weights)
     slot_ref[...] = slots
+    weight_ref[...] = weights
+
+
+def spread_gain(gain):
+    high, low = split(gain)
+    rows = (16, DH)
+    return (
+        jnp.broadcast_to(high.astype(F32), rows).astype(BF16),
+        jnp.broadcast_to(low.astype(F32), rows).astype(BF16),
+    )
+
+
+def read_gain(high, low):
+    return (high.astype(F32) + low.astype(F32))[0:1]
 
 
 def mixer_kernel(
@@ -122,29 +136,31 @@
     inclusive = (row >= col)[None]
     upper = (row <= col)[None]
     lower = (row > col)[None]
-    group = STEPS
 
     def same(size):
         return ((row // size) == (col // size))[None]
 
-    identity = jnp.broadcast_to(eye.astype(F32), (group, BLOCK, BLOCK))
-    identity_half = identity.astype(BF16)
+    identity = jnp.broadcast_to(eye.astype(F32), (GROUP, BLOCK, BLOCK))
+    wide_row = lax.broadcasted_iota(jnp.int32, (DH, DH), 0)
+    wide_col = lax.broadcasted_iota(jnp.int32, (DH, DH), 1)
+    wide_eye = jnp.broadcast_to((wide_row == wide_col).astype(F32)[None], (GROUP, DH, DH)).astype(BF16)
 
     def parts(step, unused):
-        start = step * group
-        block = recv_ref[pl.ds(start, group)]
+        start = step * GROUP
+        block = recv_ref[pl.ds(start, GROUP)]
         q = block[:, 0:64]
         k = block[:, 64:128]
-        extra = block[:, 128:192]
+        v = block[:, 128:192]
+        gates = block[:, 192:208].astype(F32)
+        decay_row = gates[:, 0:1, 0:64]
+        strength_row = gates[:, 0:1, 64:128]
         qf = q.astype(F32)
         kf = k.astype(F32)
         q_norm = lax.rsqrt(jnp.sum(qf * qf, axis=2, keepdims=True) + 1e-06)
         k_norm = lax.rsqrt(jnp.sum(kf * kf, axis=2, keepdims=True) + 1e-06)
         k_norm_row = jnp.sum(jnp.where(eye, k_norm, 0.0), axis=1, keepdims=True)
-        decay = extra[:, :, 64:65].astype(F32)
-        strength = extra[:, :, 65:66].astype(F32)
-        strength_row = jnp.sum(jnp.where(eye, strength, 0.0), axis=1, keepdims=True)
-        decay_row = jnp.sum(jnp.where(eye, decay, 0.0), axis=1, keepdims=True)
+        decay = jnp.sum(jnp.where(eye, decay_row, 0.0), axis=2, keepdims=True)
+        strength = jnp.sum(jnp.where(eye, strength_row, 0.0), axis=2, keepdims=True)
         cum_row = jnp.sum(jnp.where(upper, decay, 0.0), axis=1, keepdims=True)
         cum = jnp.sum(jnp.where(inclusive, decay_row, 0.0), axis=2, keepdims=True)
         spread = cum - cum_row
@@ -168,20 +184,20 @@
         tail = jnp.exp(last - cum)
         unit_k = k_norm * kf
         w = bdot_nn(inverse_half, ((strength * decay_gain) * unit_k).astype(BF16)).astype(BF16)
-        v_t = bdot_nt(identity_half, extra[:, :, 0:64]) * strength_row
+        v_t = bdot_nt(wide_eye, v) * strength_row
         u_t = bdot_nt(v_t.astype(BF16), inverse_half)
         scores = (query_dot * fade).astype(BF16)
         q_part = decay_gain * (q_norm * qf) - bdot_nn(scores, w)
         local = bdot_nt(scores, u_t.astype(BF16))
-        w_ref[pl.ds(start, group)] = w
-        u_ref[pl.ds(start, group)] = u_t
-        k_ref[pl.ds(start, group)] = (tail * unit_k).astype(BF16)
-        gain_ref[pl.ds(start, group)] = jnp.broadcast_to(jnp.exp(last), (group, 8, 128))
-        query_part_ref[pl.ds(start, group)] = q_part.astype(BF16)
-        local_ref[pl.ds(start, group)] = local
+        w_ref[pl.ds(start, GROUP)] = w
+        u_ref[pl.ds(start, GROUP)] = u_t
+        k_ref[pl.ds(start, GROUP)] = (tail * unit_k).astype(BF16)
+        gain_ref[pl.ds(start, GROUP)] = jnp.broadcast_to(jnp.exp(last), (GROUP, 8, 128))
+        query_part_ref[pl.ds(start, GROUP)] = q_part.astype(BF16)
+        local_ref[pl.ds(start, GROUP)] = local
         return unused
 
-    lax.fori_loop(0, BLOCKS // group, parts, 0)
+    lax.fori_loop(0, BLOCKS // GROUP, parts, 0)
 
     map_row = lax.broadcasted_iota(jnp.int32, (MAP_ROWS, DH), 0)
     map_col = lax.broadcasted_iota(jnp.int32, (MAP_ROWS, DH), 1)
@@ -227,32 +243,89 @@
             whole = gain * whole + dot_nn(whole.astype(BF16), changed[0:DH].astype(BF16)) + added
             total = gain * total
     send_ref[0:MAP_ROWS, :] = (whole - jnp.where(diagonal, total, 0.0)).astype(BF16)
-    high, low = split(total)
-    send_ref[MAP_ROWS : MAP_ROWS + 16, :] = jnp.broadcast_to(high.astype(F32), (16, DH)).astype(BF16)
-    send_ref[MAP_ROWS + 16 : MAP_ROWS + 32, :] = jnp.broadcast_to(low.astype(F32), (16, DH)).astype(BF16)
-
-
-def fold_kernel(
-    position_ref, maps_ref, query_part_ref, local_ref, sub_map_ref, sub_gain_ref, out_ref
-):
+    high, low = spread_gain(total)
+    send_ref[MAP_ROWS : MAP_ROWS + 16, :] = high
+    send_ref[MAP_ROWS + 16 : MAP_ROWS + 32, :] = low
+
+
+def compose_kernel(half_ref, own_ref, other_ref, out_ref):
+    map_row = lax.broadcasted_iota(jnp.int32, (MAP_ROWS, DH), 0)
+    map_col = lax.broadcasted_iota(jnp.int32, (MAP_ROWS, DH), 1)
+    diagonal = map_row == map_col
+
+    def emit(first_ref, second_ref, start):
+        gain_first = read_gain(first_ref[MAP_ROWS : MAP_ROWS + 16], first_ref[MAP_ROWS + 16 : MAP_ROWS + 32])
+        gain = read_gain(second_ref[MAP_ROWS : MAP_ROWS + 16], second_ref[MAP_ROWS + 16 : MAP_ROWS + 32])
+        total = gain * gain_first
+        first = first_ref[0:MAP_ROWS, :].astype(F32) + jnp.where(diagonal, gain_first, 0.0)
+        second = second_ref[0:MAP_ROWS, :].astype(F32)
+        whole = gain * first + dot_nn(first.astype(BF16), second_ref[0:DH, :])
+        whole = whole + jnp.where(map_row < DH, 0.0, second) - jnp.where(diagonal, total, 0.0)
+        out_ref[0:DH, :] = whole[0:DH].astype(BF16)
+        out_ref[DH : DH + WIDTH, :] = whole[DH + start : DH + start + WIDTH].astype(BF16)
+        high, low = spread_gain(total)
+        out_ref[DH + WIDTH : DH + WIDTH + 16, :] = high
+        out_ref[DH + WIDTH + 16 : DH + WIDTH + 32, :] = low
+
+    @pl.when(half_ref[0] == 0)
+    def _():
+        emit(own_ref, other_ref, 0)
+
+    @pl.when(half_ref[0] != 0)
+    def _():
+        emit(other_ref, own_ref, WIDTH)
+
+
+def fold_kernel(position_ref, maps_ref, out_ref):
     def fold(index, state):
-        gain = (
-            maps_ref[index, MAP_ROWS : MAP_ROWS + 16, :].astype(F32)
-            + maps_ref[index, MAP_ROWS + 16 : MAP_ROWS + 32, :].astype(F32)
-        )[0:1]
+        gain = read_gain(
+            maps_ref[index, DH + WIDTH : DH + WIDTH + 16, :],
+            maps_ref[index, DH + WIDTH + 16 : DH + WIDTH + 32, :],
+        )
         return (
             gain * state
             + dot_nn(state.astype(BF16), maps_ref[index, 0:DH, :])
-            + maps_ref[index, DH:MAP_ROWS, :].astype(F32)
+            + maps_ref[index, DH : DH + WIDTH, :].astype(F32)
         )
 
-    state = lax.fori_loop(0, position_ref[0], fold, jnp.zeros((WIDTH, DH), F32))
+    out_ref[...] = lax.fori_loop(0, position_ref[0], fold, jnp.zeros((WIDTH, DH), F32))
+
+
+def head_kernel(
+    half_ref,
+    own_ref,
+    other_ref,
+    other_map_ref,
+    query_part_ref,
+    local_ref,
+    sub_map_ref,
+    sub_gain_ref,
+    out_ref,
+    state_ref,
+):
+    @pl.when(half_ref[0] == 0)
+    def _():
+        state_ref[0:WIDTH, :] = own_ref[...]
+        state_ref[WIDTH:DH, :] = other_ref[...]
+
+    @pl.when(half_ref[0] != 0)
+    def _():
+        state = jnp.concatenate([other_ref[...], own_ref[...]], axis=0)
+        gain = read_gain(
+            other_map_ref[MAP_ROWS : MAP_ROWS + 16, :], other_map_ref[MAP_ROWS + 16 : MAP_ROWS + 32, :]
+        )
+        state_ref[...] = (
+            gain * state
+            + dot_nn(state.astype(BF16), other_map_ref[0:DH, :])
+            + other_map_ref[DH:MAP_ROWS, :].astype(F32)
+        )
+
+    state = state_ref[...]
     for chunk in range(CHUNKS):
         half = state.astype(BF16)
         for step in range(STEPS):
             index = chunk * STEPS + step
-            out = dot_nt(query_part_ref[index], half) + local_ref[index]
-            out_ref[index] = jnp.concatenate([out[0:32], out[32:64]], axis=1).astype(BF16)
+            out_ref[index] = (dot_nt(query_part_ref[index], half) + local_ref[index]).astype(BF16)
         if chunk + 1 < CHUNKS:
             changed = sub_map_ref[chunk]
             state = (
@@ -265,15 +338,10 @@
 def mixed_kernel(
     tok_ref, heads_ref, residual_ref, out_gain_ref, ffn_gain_ref, mixed_ref, send_ref, rows_ref
 ):
-    lane = lax.broadcasted_iota(jnp.int32, (32, 128), 1)
     gain = out_gain_ref[...]
     total = jnp.zeros((TOK, 1), F32)
     for head in range(VALUE_HEADS):
-        left = heads_ref[2 * head].astype(F32)
-        right = heads_ref[2 * head + 1].astype(F32)
-        top = jnp.where(lane < 64, left, pltpu.roll(right, 64, 1))
-        bottom = jnp.where(lane < 64, pltpu.roll(left, 64, 1), right)
-        wide = jnp.concatenate([top, bottom], axis=0)
+        wide = heads_ref[head].astype(F32)
         scale = lax.rsqrt(jnp.mean(wide * wide, axis=1, keepdims=True) + 1e-06)
         part = slice(head * DH, head * DH + DH)
         mixed = (residual_ref[:, part].astype(F32) + wide * scale * gain).astype(BF16)
@@ -305,24 +373,27 @@
 
 def expert_kernel(rows_ref, gate_ref, up_ref, down_ref, out_ref, wide_ref):
     swap = swap_matrix()
-    for group in range(FFN_ROWS // 16):
-        tile = dot_nn(swap, rows_ref[group * 256 : group * 256 + 256, :]).astype(BF16)
+    for pair in range(FFN_ROWS // 32):
+        start = pair * 512
+        rows = [rows_ref[start : start + 256, :], rows_ref[start + 256 : start + 512, :]]
+        tile = dot_nn(swap, jnp.concatenate(rows, axis=1)).astype(BF16)
         for c in range(COLS):
-            wide_ref[group * 16 : group * 16 + 16, c * 128 : c * 128 + 128] = tile[
-                c * 16 : c * 16 + 16
-            ]
+            part = slice(c * 128, c * 128 + 128)
+            wide_ref[pair * 32 : pair * 32 + 16, part] = tile[c * 16 : c * 16 + 16, 0:128]
+            wide_ref[pair * 32 + 16 : pair * 32 + 32, part] = tile[c * 16 : c * 16 + 16, 128:256]
     wide = wide_ref[...]
     gate = dot_nn(wide, gate_ref[...])
     up = dot_nn(wide, up_ref[...])
     hidden = (gate / (1.0 + jnp.exp(-gate)) * up).astype(BF16)
     wide_ref[...] = dot_nn(hidden, down_ref[...]).astype(BF16)
-    for group in range(FFN_ROWS // 16):
-        pieces = [
-            wide_ref[group * 16 : group * 16 + 16, c * 128 : c * 128 + 128] for c in range(COLS)
-        ]
-        out_ref[group * 256 : group * 256 + 256, :] = dot_nn(
-            swap, jnp.concatenate(pieces, axis=0)
-        ).astype(BF16)
+    for pair in range(FFN_ROWS // 32):
+        sides = []
+        for start in (pair * 32, pair * 32 + 16):
+            pieces = [wide_ref[start : start + 16, c * 128 : c * 128 + 128] for c in range(COLS)]
+            sides.append(jnp.concatenate(pieces, axis=0))
+        tile = dot_nn(swap, jnp.concatenate(sides, axis=1)).astype(BF16)
+        out_ref[pair * 512 : pair * 512 + 256, :] = tile[:, 0:128]
+        out_ref[pair * 512 + 256 : pair * 512 + 512, :] = tile[:, 128:256]
 
 
 def combine_kernel(slot_ref, weight_ref, rows_ref, out_ref, sum_ref):
@@ -353,7 +424,7 @@
 def pack(query, key, value, decay, strength):
     return pl.pallas_call(
         pack_kernel,
-        out_shape=shape((LANES, 192, 128), BF16),
+        out_shape=shape((VALUE_HEADS, PACK_ROWS, 128), BF16),
         in_specs=[WHOLE] * 5,
         out_specs=WHOLE,
         compiler_params=params(),
@@ -361,15 +432,19 @@
     )(query, key, value, decay, strength)
 
 
-def route(ids):
+def route(ids, weights):
     return pl.pallas_call(
         route_kernel,
-        out_shape=(shape((2, EXPERTS), jnp.int32), shape((TOK, 128), jnp.int32)),
-        in_specs=[WHOLE],
-        out_specs=(WHOLE, WHOLE),
+        out_shape=(
+            shape((2, EXPERTS), jnp.int32),
+            shape((TOK, 128), jnp.int32),
+            shape((TOK, 128), F32),
+        ),
+        in_specs=[WHOLE, WHOLE],
+        out_specs=(WHOLE, WHOLE, WHOLE),
         compiler_params=params(),
         name="route",
-    )(ids)
+    )(ids, weights)
 
 
 def mixer(received):
@@ -377,16 +452,16 @@
         mixer_kernel,
         out_shape=(
             shape((BLOCKS, BLOCK, DH), BF16),
-            shape((BLOCKS, BLOCK, WIDTH), F32),
+            shape((BLOCKS, BLOCK, DH), F32),
             shape((CHUNKS, MAP_ROWS, DH), F32),
             shape((CHUNKS, 8, DH), F32),
-            shape((MAP_ROWS + 32, DH), BF16),
+            shape((HALF_ROWS, DH), BF16),
         ),
         in_specs=[WHOLE],
         out_specs=(WHOLE,) * 5,
         scratch_shapes=[
             pltpu.VMEM((BLOCKS, BLOCK, DH), BF16),
-            pltpu.VMEM((BLOCKS, WIDTH, BLOCK), F32),
+            pltpu.VMEM((BLOCKS, DH, BLOCK), F32),
             pltpu.VMEM((BLOCKS, BLOCK, DH), BF16),
             pltpu.VMEM((BLOCKS, 8, DH), F32),
         ],
@@ -395,15 +470,38 @@
     )(received)
 
 
-def fold(position, maps, query_part, local, sub_map, sub_gain):
+def compose(half, own, other):
+    return pl.pallas_call(
+        compose_kernel,
+        out_shape=shape((SEG_ROWS, DH), BF16),
+        in_specs=[SMEM, WHOLE, WHOLE],
+        out_specs=WHOLE,
+        compiler_params=params(),
+        name="compose",
+    )(half, own, other)
+
+
+def fold(position, maps):
     return pl.pallas_call(
         fold_kernel,
-        out_shape=shape((BLOCKS, 32, 128), BF16),
-        in_specs=[SMEM] + [WHOLE] * 5,
+        out_shape=shape((WIDTH, DH), F32),
+        in_specs=[SMEM, WHOLE],
         out_specs=WHOLE,
         compiler_params=params(),
         name="fold",
-    )(position, maps, query_part, local, sub_map, sub_gain)
+    )(position, maps)
+
+
+def head_rows(half, own, other, other_map, query_part, local, sub_map, sub_gain):
+    return pl.pallas_call(
+        head_kernel,
+        out_shape=shape((BLOCKS, BLOCK, DH), BF16),
+        in_specs=[SMEM] + [WHOLE] * 7,
+        out_specs=WHOLE,
+        scratch_shapes=[pltpu.VMEM((DH, DH), F32)],
+        compiler_params=params(),
+        name="heads",
+    )(half, own, other, other_map, query_part, local, sub_map, sub_gain)
 
 
 def mix(tok, heads, residual, out_gain, ffn_gain):
@@ -452,6 +550,15 @@
 
 def swap_all(x, axes):
     return lax.all_to_all(x, axes, split_axis=0, concat_axis=0, tiled=True)
+
+
+def trade(x):
+    return lax.ppermute(x, "half", [(0, 1), (1, 0)])
+
+
+HEAD_AXES = ("pair", "y")
+SEQ_AXES = ("half", "pair", "y")
+EXP_AXES = ("z", "core")
 
 
 def body(
@@ -469,30 +576,35 @@
     up_proj,
     down_proj,
 ):
-    sent = pack(mixer_query[0], mixer_key[0], mixer_value[0], log_decay[0], strength[0])
-    received = swap_all(sent, "seq")
-    tok, slots = route(expert_ids[0])
+    sent = pack(mixer_query[0], mixer_key[0], mixer_value[0], log_decay[0].T, strength[0].T)
+    received = swap_all(sent, HEAD_AXES)
+    tok, slots, weights = route(expert_ids[0], expert_weights[0])
+    half = lax.axis_index("half").astype(jnp.int32).reshape(1)
+    position = lax.axis_index(EXP_AXES).astype(jnp.int32).reshape(1)
     query_part, local, sub_map, sub_gain, own_map = mixer(received)
-    maps = lax.all_gather(own_map, "exp", axis=0)
-    position = lax.axis_index("exp").astype(jnp.int32).reshape(1)
-    head_rows = fold(position, maps, query_part, local, sub_map, sub_gain)
-    heads = swap_all(head_rows, "seq")
+    other_map = trade(own_map)
+    maps = lax.all_gather(compose(half, own_map, other_map), EXP_AXES, axis=0)
+    own_state = fold(position, maps)
+    other_state = trade(own_state)
+    outs = head_rows(half, own_state, other_state, other_map, query_part, local, sub_map, sub_gain)
+    heads = swap_all(outs, HEAD_AXES)
     mixed, outgoing = mix(
         tok, heads, residual[0], out_gain.reshape(1, DH), ffn_gain.reshape(1, D)
     )
-    arrived = swap_all(outgoing, ("seq", "exp"))
+    arrived = swap_all(outgoing, SEQ_AXES + EXP_AXES)
     result = experts(arrived.reshape(SLOTS * 16, 128), gate_proj[0], up_proj[0], down_proj[0])
-    returned = swap_all(result.reshape(SLOTS, 16, 128), ("seq", "exp"))
-    ffn_out = combine(slots, expert_weights[0], returned)
+    returned = swap_all(result.reshape(SLOTS, 16, 128), SEQ_AXES + EXP_AXES)
+    ffn_out = combine(slots, weights, returned)
     return (mixed[None], ffn_out[None])
 
 
 def solution(mesh):
-    rows = P("exp", "seq", None)
-    owned = P(("seq", "exp"), None, None)
+    fine = Mesh(mesh.devices.reshape(2, 2, 8, 8, 2), SEQ_AXES + EXP_AXES)
+    rows = P(EXP_AXES, SEQ_AXES, None)
+    owned = P(SEQ_AXES + EXP_AXES, None, None)
     return jax.shard_map(
         body,
-        mesh=mesh,
+        mesh=fine,
         in_specs=(rows,) * 6 + (P(), P(), rows, rows) + (owned,) * 3,
         out_specs=(rows, rows),
         check_vma=False,

time: 366 us -> 335 us (0.915)
  blocking collectives: 141 us -> 279 us
  waiting for transfers between devices: 139 us -> 9.64 us
  Pallas kernels: 50.2 us -> 27.4 us
  starting transfers between devices: 28.6 us -> 13.2 us
    all_to_all x1 -> x3, blocking collectives: 111 us -> 250 us  [swap_all(): return lax.all_to_all(x, axes, split_axis=0, concat_axis=0, tiled=True)]
    all_to_all x3 -> x1, waiting for transfers between devices: 139 us -> 5.63 us  [swap_all(): return lax.all_to_all(x, axes, split_axis=0, concat_axis=0, tiled=True)]
    all_to_all x3 -> x1, starting transfers between devices: 28.6 us -> 4.42 us  [swap_all(): return lax.all_to_all(x, axes, split_axis=0, concat_axis=0, tiled=True)]
    pallas_call x1, Pallas kernels: 17.9 us -> 8.54 us  [mixer(): pl.pallas_call(mixer_kernel, out_shape=(shape((BLOCKS, BLOCK, DH), BF16),...]
    ppermute x0 -> x2, starting transfers between devices: none -> 8.73 us  [trade(): return lax.ppermute(x, 'half', [(0, 1), (1, 0)])]
    pallas_call x1, Pallas kernels: 12.3 us -> 7.19 us  [experts(): pl.pallas_call(expert_kernel, grid=(SLOTS // FFN_ROWS,), out_shape=shape(...]
    pallas_call x2 -> x4, Pallas kernels: 6.35 us -> 1.95 us  [the longest x1 1.54 us: head_rows(): pl.pallas_call(head_kernel, out_shape=shape((BLOCKS, BLOCK, DH), BF16), i...]
    ppermute x0 -> x2, waiting for transfers between devices: none -> 4 us  [trade(): return lax.ppermute(x, 'half', [(0, 1), (1, 0)])]
where the time goes in v2:
time: 335 us; the launch traced here: 334 us
  blocking collectives  279 us (83%)
  Pallas kernels  27.4 us (8%)
  starting transfers between devices  13.2 us (4%)
  waiting for transfers between devices  9.64 us (3%)
  local copies, waits for them, and re-layouts  4.35 us (1%)
    all_to_all x3, blocking collectives, swap_all(): return lax.all_to_all(x, axes, split_axis=0, concat_axis=0, tiled=True)  250 us
    all_gather x1, blocking collectives, body(): maps = lax.all_gather(compose(half, own_map, other_map), EXP_AXES, axis=0)  28.9 us
    ppermute x2, starting transfers between devices, trade(): return lax.ppermute(x, 'half', [(0, 1), (1, 0)])  8.73 us
    pallas_call x1, Pallas kernels, mixer(): pl.pallas_call(mixer_kernel, out_shape=(shape((BLOCKS, BLOCK, DH), BF16),...  8.54 us
    pallas_call x1, Pallas kernels, experts(): pl.pallas_call(expert_kernel, grid=(SLOTS // FFN_ROWS,), out_shape=shape(...  7.19 us
  transfers between devices with their start and end apart: 3, of which 3 were waited for; matrix products, arithmetic and copies ran while one was open for 0% of the time, Pallas kernels for 1%

profile of v2, /device:TPU:1, one launch (start us, length us, event | category | flops | bytes accessed | tf_op | source)
XLA Modules:
  0.0 334.5 jit_solution(9066437977266044368)
XLA Ops:
  0.6 0.0 copy-start.11
  0.6 0.0 copy-start.4
  0.7 0.9 copy-done.4
  1.6 0.0 copy-start.5
  1.6 0.9 copy-done.5
  2.5 0.0 copy-start.6
  2.5 0.9 copy-done.6
  3.4 0.0 copy-start.8
  3.4 0.7 copy-done.8
  4.1 0.0 copy-start.9
  4.1 0.7 copy-done.9
  4.8 0.0 copy-start.12
  4.8 0.0 copy-start.3
  4.8 0.0 copy-start.7
  4.8 0.0 copy-start.10
  4.8 0.1 pack.1
  4.9 29.8 %all_to_all.20.recv_ref = bf16[16,208,128]{2,1,0:T(8,128)(2,1)S(1)} all-to-all(bf16[16,208,128]{2,1,0:T(8,128)(2,1)S(1)} %pack.1), channel_id=1, replica_groups=mesh['half'=2,'pair'=2,'y'=8,'z'=8,'core'=2] {'pair','y'}, dimensions={0} | all-to-all | bytes 1703936 | tf_op jit(solution)/shard_map/all_to_all | solution.py:552
  34.7 8.5 %mixer.1 = (bf16[16,64,128]{2,1,0:T(8,128)(2,1)S(1)}, f32[16,64,128]{2,1,0:T(8,128)S(1)}, f32[4,256,128]{2,1,0:T(8,128)S(1)}, f32[4,8,128]{2,1,0:T(8,128)S(1)}, bf16[288,128]{1,0:T(8,128)(2,1)S(1)}) custom-call(bf16[16,208,128]{2,1,0:T(8,128)(2,1)S(1)} %all_to_all.20.recv_ref), custom_call_target="tpu_custom_call" | custom-call | tf_op jit(solution)/shard_map/mixer/pallas_call | solution.py:451
  43.2 4.4 %collective-permute-start = (bf16[288,128]{1,0:T(8,128)(2,1)S(1)}, bf16[288,128]{1,0:T(8,128)(2,1)S(1)}, u32[]{:S(2)}, u32[]{:S(2)}) collective-permute-start(bf16[288,128]{1,0:T(8,128)(2,1)S(1)} %get-tuple-element.13.own_ref), channel_id=1, source_target_pairs={{0,256},{256,0},{1,257},{257,1},{2,258},{258,2},{3,259},{259,3},{4... | collective-permute-start | bytes 221192 | tf_op jit(solution)/shard_map/ppermute | solution.py:556
  47.6 2.2 collective-permute-done.other_ref.other_map_ref
  49.8 0.2 compose.1
  50.0 28.9 %all-gather = bf16[3584,128]{1,0:T(8,128)(2,1)S(1)} all-gather(bf16[224,128]{1,0:T(8,128)(2,1)S(1)} %compose.1), channel_id=2, replica_groups=mesh['half'=2,'pair'=2,'y'=8,'z'=8,'core'=2] {'z','core'}, dimensions={0}, use_global_device_ids=true | all-gather | bytes 974848 | tf_op jit(solution)/shard_map/all_gather | solution.py:586
  78.9 0.1 fold.1.own_ref
  79.0 4.4 %collective-permute-start.1 = (f32[64,128]{1,0:T(8,128)S(1)}, f32[64,128]{1,0:T(8,128)S(1)}, u32[]{:S(2)}, u32[]{:S(2)}) collective-permute-start(f32[64,128]{1,0:T(8,128)S(1)} %fold.1.own_ref), channel_id=1, source_target_pairs={{0,256},{256,0},{1,257},{257,1},{2,258},{258,2},{3,259},{259,3},{4... | collective-permute-start | bytes 98312 | tf_op jit(solution)/shard_map/ppermute | solution.py:556
  83.4 1.8 collective-permute-done.1.other_ref
  85.2 1.5 heads.1
  86.7 4.4 %all-to-all-start.1 = ((bf16[16,64,128]{2,1,0:T(8,128)(2,1)}), bf16[16,64,128]{2,1,0:T(8,128)(2,1)S(1)}, u32[]{:S(2)}, u32[]{:S(2)}) async-start(bf16[16,64,128]{2,1,0:T(8,128)(2,1)} %heads.1), calls=%async_computation.1 | async-start | bytes 524288 | tf_op jit(solution)/shard_map/all_to_all | solution.py:552
  91.2 0.0 copy-done.11
  91.2 0.1 copy.15
  91.3 0.0 copy-done.12
  91.3 0.1 copy.16
  91.4 2.1 route.1
  93.4 5.6 %all-to-all-done.1.heads_ref = bf16[16,64,128]{2,1,0:T(8,128)(2,1)S(1)} async-done(((bf16[16,64,128]{2,1,0:T(8,128)(2,1)}), bf16[16,64,128]{2,1,0:T(8,128)(2,1)S(1)}, u32[]{:S(2)}, u32[]{:S(2)}) %all-to-all-start.1) | async-done | bytes 262176 | tf_op jit(solution)/shard_map/all_to_all | solution.py:552
  99.1 0.0 copy-done.3
  99.1 0.0 copy-done.7
  99.1 0.0 copy-done.10
  99.1 3.9 %mix.1 = (bf16[64,2048]{1,0:T(8,128)(2,1)}, bf16[1024,16,128]{2,1,0:T(8,128)(2,1)S(1)}) custom-call(s32[2,512]{1,0:T(2,128)S(1)} %get-tuple-element.12.tok_ref, bf16[16,64,128]{2,1,0:T(8,128)(2,1)S(1)} %all-to-all-done.1.heads_ref, bf16[64,2048]{1,0:T(8,128)(2,1)S(1)} %bitcast.30, f32[1,128]{1,0:T(1,128)S(1)} %bitcast.39, f32[1,2048]{1,0:T(1,128)S(1)} %bitcast.36), custom_call_target="tpu_custom_call" | custom-call | tf_op jit(solution)/shard_map/mix/pallas_call | solution.py:508
  103.0 0.0 copy-start
  103.0 0.0 copy-start.1
  103.0 0.0 copy-start.2
  103.0 112.2 %all_to_all.21 = bf16[1024,16,128]{2,1,0:T(8,128)(2,1)S(1)} all-to-all(bf16[1024,16,128]{2,1,0:T(8,128)(2,1)S(1)} %get-tuple-element.21), channel_id=1, replica_groups=mesh['half'=2,'pair'=2,'y'=8,'z'=8,'core'=2] {'half','pair','y','z','core'}, dimensions={0} | all-to-all | bytes 8388608 | tf_op jit(solution)/shard_map/all_to_all | solution.py:552
  215.1 0.0 copy-done
  215.1 0.0 copy-done.1
  215.1 0.0 copy-done.2
  215.2 7.2 %experts.1 = bf16[16384,128]{1,0:T(8,128)(2,1)S(1)} custom-call(bf16[16384,128]{1,0:T(8,128)(2,1)S(1)} %bitcast.24, bf16[2048,256]{1,0:T(8,128)(2,1)S(1)} %bitcast.27, bf16[2048,256]{1,0:T(8,128)(2,1)S(1)} %bitcast.28, bf16[256,2048]{1,0:T(8,128)(2,1)S(1)} %bitcast.29), custom_call_target="tpu_custom_call" | custom-call | tf_op jit(solution)/shard_map/experts/pallas_call | solution.py:522
  222.3 108.4 %all_to_all.22.rows_ref = bf16[1024,16,128]{2,1,0:T(8,128)(2,1)S(1)} all-to-all(bf16[1024,16,128]{2,1,0:T(8,128)(2,1)S(1)} %bitcast.25), channel_id=1, replica_groups=mesh['half'=2,'pair'=2,'y'=8,'z'=8,'core'=2] {'half','pair','y','z','core'}, dimensions={0} | all-to-all | bytes 8388608 | tf_op jit(solution)/shard_map/all_to_all | solution.py:552
  330.8 3.7 %combine.1 = bf16[64,2048]{1,0:T(8,128)(2,1)} custom-call(s32[64,128]{1,0:T(8,128)S(1)} %get-tuple-element.19.slot_ref, f32[64,128]{1,0:T(8,128)S(1)} %get-tuple-element.20.weight_ref, bf16[1024,16,128]{2,1,0:T(8,128)(2,1)S(1)} %all_to_all.22.rows_ref), custom_call_target="tpu_custom_call" | custom-call | tf_op jit(solution)/shard_map/combine/pallas_call | solution.py:540
Async XLA Ops:
  0.6 90.5 %copy-start.11 = (s32[1,64,10]{1,0,2:T(1,128)S(1)}, s32[1,64,10]{1,0,2:T(1,128)}, u32[]{:S(2)}) copy-start(s32[1,64,10]{1,0,2:T(1,128)} %param.21) | copy-start | bytes 7684
  0.6 1.0 copy-start.4
  1.6 0.9 copy-start.5
  2.5 0.9 copy-start.6
  3.4 0.7 copy-start.8
  4.1 0.7 copy-start.9
  4.8 86.5 %copy-start.12 = (f32[1,64,10]{1,0,2:T(1,128)S(1)}, f32[1,64,10]{1,0,2:T(1,128)}, u32[]{:S(2)}) copy-start(f32[1,64,10]{1,0,2:T(1,128)} %param.22) | copy-start | bytes 7684
  4.8 94.3 %copy-start.3 = (bf16[1,64,2048]{2,1,0:T(8,128)(2,1)S(1)}, bf16[1,64,2048]{2,1,0:T(8,128)(2,1)}, u32[]{:S(2)}) copy-start(bf16[1,64,2048]{2,1,0:T(8,128)(2,1)} %param.18) | copy-start | bytes 786436
  4.8 94.3 %copy-start.7 = (f32[2048]{0:T(1024)S(1)}, f32[2048]{0:T(1024)}, u32[]{:S(2)}) copy-start(f32[2048]{0:T(1024)} %param.20) | copy-start | bytes 24580
  4.8 94.3 %copy-start.10 = (f32[128]{0:T(128)S(1)}, f32[128]{0:T(128)}, u32[]{:S(2)}) copy-start(f32[128]{0:T(128)} %param.19) | copy-start | bytes 1540
  43.2 6.6 %collective-permute-start = (bf16[288,128]{1,0:T(8,128)(2,1)S(1)}, bf16[288,128]{1,0:T(8,128)(2,1)S(1)}, u32[]{:S(2)}, u32[]{:S(2)}) collective-permute-start(bf16[288,128]{1,0:T(8,128)(2,1)S(1)} %get-tuple-element.13.own_ref), channel_id=1, source_target_pairs={{0,256},{256,0},{1,257},{257,1},{2,258},{258,2},{3,259},{259,3},{4... | collective-permute-start | bytes 221192 | tf_op jit(solution)/shard_map/ppermute | solution.py:556
  79.0 6.2 %collective-permute-start.1 = (f32[64,128]{1,0:T(8,128)S(1)}, f32[64,128]{1,0:T(8,128)S(1)}, u32[]{:S(2)}, u32[]{:S(2)}) collective-permute-start(f32[64,128]{1,0:T(8,128)S(1)} %fold.1.own_ref), channel_id=1, source_target_pairs={{0,256},{256,0},{1,257},{257,1},{2,258},{258,2},{3,259},{259,3},{4... | collective-permute-start | bytes 98312 | tf_op jit(solution)/shard_map/ppermute | solution.py:556
  86.7 12.3 %all-to-all-start.1 = ((bf16[16,64,128]{2,1,0:T(8,128)(2,1)}), bf16[16,64,128]{2,1,0:T(8,128)(2,1)S(1)}, u32[]{:S(2)}, u32[]{:S(2)}) async-start(bf16[16,64,128]{2,1,0:T(8,128)(2,1)} %heads.1), calls=%async_computation.1 | async-start | bytes 524288 | tf_op jit(solution)/shard_map/all_to_all | solution.py:552
  103.0 112.2 %copy-start = (bf16[1,2048,256]{2,1,0:T(8,128)(2,1)S(1)}, bf16[1,2048,256]{2,1,0:T(8,128)(2,1)}, u32[]{:S(2)}) copy-start(bf16[1,2048,256]{2,1,0:T(8,128)(2,1)} %param.23) | copy-start | bytes 3145732
  103.0 112.2 %copy-start.1 = (bf16[1,2048,256]{2,1,0:T(8,128)(2,1)S(1)}, bf16[1,2048,256]{2,1,0:T(8,128)(2,1)}, u32[]{:S(2)}) copy-start(bf16[1,2048,256]{2,1,0:T(8,128)(2,1)} %param.24) | copy-start | bytes 3145732
  103.0 112.2 %copy-start.2 = (bf16[1,256,2048]{2,1,0:T(8,128)(2,1)S(1)}, bf16[1,256,2048]{2,1,0:T(8,128)(2,1)}, u32[]{:S(2)}) copy-start(bf16[1,256,2048]{2,1,0:T(8,128)(2,1)} %param.25) | copy-start | bytes 3145732

commit v3 on v2

--- a/solution.py
+++ b/solution.py
@@ -27,7 +27,7 @@
 COLS = D // 128
 F32 = jnp.float32
 BF16 = jnp.bfloat16
-VMEM_LIMIT = 28 * 1024 * 1024
+VMEM_LIMIT = 16 * 1024 * 1024
 
 
 def params():
@@ -71,14 +71,45 @@
     return (in_index == (out_index % 16) * 16 + out_index // 16).astype(BF16)
 
 
-def pack_kernel(query_ref, key_ref, value_ref, decay_ref, strength_ref, out_ref):
-    gates = jnp.concatenate([decay_ref[...].astype(F32), strength_ref[...].astype(F32)], axis=1)
+def pack_kernel(
+    half_ref,
+    query_ref,
+    key_ref,
+    value_ref,
+    decay_ref,
+    strength_ref,
+    out_ref,
+    decay_rows,
+    strength_rows,
+    sems,
+):
+    gate_copies = [
+        pltpu.make_async_copy(decay_ref, decay_rows, sems.at[3, 0]),
+        pltpu.make_async_copy(strength_ref, strength_rows, sems.at[3, 1]),
+    ]
+    copies = []
     for head in range(VALUE_HEADS):
-        shared = slice(head // 2 * DH, head // 2 * DH + DH)
-        out_ref[head, 0:64, :] = query_ref[:, shared]
-        out_ref[head, 64:128, :] = key_ref[:, shared]
-        out_ref[head, 128:192, :] = value_ref[:, head * DH : head * DH + DH]
-        out_ref[head, 192:208, :] = jnp.broadcast_to(gates[head : head + 1], (16, 128)).astype(BF16)
+        place = lax.rem(head + half_ref[0] * 8, VALUE_HEADS)
+        for part, (ref, column) in enumerate(
+            ((query_ref, head // 2), (key_ref, head // 2), (value_ref, head))
+        ):
+            copies.append(
+                pltpu.make_async_copy(
+                    ref.at[:, column * DH : column * DH + DH],
+                    out_ref.at[place, part * TOK : part * TOK + TOK, :],
+                    sems.at[part, head],
+                )
+            )
+    for copy in gate_copies + copies:
+        copy.start()
+    for copy in gate_copies:
+        copy.wait()
+    gates = jnp.concatenate([decay_rows[...].astype(F32), strength_rows[...].astype(F32)], axis=1)
+    for head in range(VALUE_HEADS):
+        place = lax.rem(head + half_ref[0] * 8, VALUE_HEADS)
+        out_ref[place, 192:208, :] = jnp.broadcast_to(gates[head : head + 1], (16, 128)).astype(BF16)
+    for copy in copies:
+        copy.wait()
 
 
 def route_kernel(ids_ref, weight_in_ref, tok_ref, slot_ref, weight_ref):
@@ -120,6 +151,9 @@
 
 def mixer_kernel(
     recv_ref,
+    next_gate_ref,
+    next_up_ref,
+    next_down_ref,
     query_part_ref,
     local_ref,
     sub_map_ref,
@@ -336,12 +370,20 @@
 
 
 def mixed_kernel(
-    tok_ref, heads_ref, residual_ref, out_gain_ref, ffn_gain_ref, mixed_ref, send_ref, rows_ref
+    half_ref,
+    tok_ref,
+    heads_ref,
+    residual_ref,
+    out_gain_ref,
+    ffn_gain_ref,
+    mixed_ref,
+    send_ref,
+    rows_ref,
 ):
     gain = out_gain_ref[...]
     total = jnp.zeros((TOK, 1), F32)
     for head in range(VALUE_HEADS):
-        wide = heads_ref[head].astype(F32)
+        wide = heads_ref[lax.rem(head + half_ref[0] * 8, VALUE_HEADS)].astype(F32)
         scale = lax.rsqrt(jnp.mean(wide * wide, axis=1, keepdims=True) + 1e-06)
         part = slice(head * DH, head * DH + DH)
         mixed = (residual_ref[:, part].astype(F32) + wide * scale * gain).astype(BF16)
@@ -369,31 +411,45 @@
 
 
 FFN_ROWS = 256
-
-
-def expert_kernel(rows_ref, gate_ref, up_ref, down_ref, out_ref, wide_ref):
+CHIPS = EXPERTS // 2
+
+
+def expert_kernel(core_ref, rows_ref, *refs):
+    weight_refs, (out_ref, wide_ref) = refs[:6], refs[6:]
     swap = swap_matrix()
+
+    def spread(start):
+        return rows_ref[start : start + 8].reshape(256, 128)
+
     for pair in range(FFN_ROWS // 32):
-        start = pair * 512
-        rows = [rows_ref[start : start + 256, :], rows_ref[start + 256 : start + 512, :]]
+        rows = [spread(pair * 16), spread(pair * 16 + 8)]
         tile = dot_nn(swap, jnp.concatenate(rows, axis=1)).astype(BF16)
         for c in range(COLS):
             part = slice(c * 128, c * 128 + 128)
             wide_ref[pair * 32 : pair * 32 + 16, part] = tile[c * 16 : c * 16 + 16, 0:128]
             wide_ref[pair * 32 + 16 : pair * 32 + 32, part] = tile[c * 16 : c * 16 + 16, 128:256]
-    wide = wide_ref[...]
-    gate = dot_nn(wide, gate_ref[...])
-    up = dot_nn(wide, up_ref[...])
-    hidden = (gate / (1.0 + jnp.exp(-gate)) * up).astype(BF16)
-    wide_ref[...] = dot_nn(hidden, down_ref[...]).astype(BF16)
+
+    def expert(gate_ref, up_ref, down_ref):
+        wide = wide_ref[...]
+        gate = dot_nn(wide, gate_ref[...])
+        up = dot_nn(wide, up_ref[...])
+        hidden = (gate / (1.0 + jnp.exp(-gate)) * up).astype(BF16)
+        wide_ref[...] = dot_nn(hidden, down_ref[...]).astype(BF16)
+
+    for which in range(2):
+
+        @pl.when(pl.program_id(0) == which)
+        def _(which=which):
+            expert(*weight_refs[which * 3 : which * 3 + 3])
+
     for pair in range(FFN_ROWS // 32):
         sides = []
         for start in (pair * 32, pair * 32 + 16):
             pieces = [wide_ref[start : start + 16, c * 128 : c * 128 + 128] for c in range(COLS)]
             sides.append(jnp.concatenate(pieces, axis=0))
         tile = dot_nn(swap, jnp.concatenate(sides, axis=1)).astype(BF16)
-        out_ref[pair * 512 : pair * 512 + 256, :] = tile[:, 0:128]
-        out_ref[pair * 512 + 256 : pair * 512 + 512, :] = tile[:, 128:256]
+        out_ref[pair * 16 : pair * 16 + 8] = tile[:, 0:128].reshape(8, 1, 32, 128)
+        out_ref[pair * 16 + 8 : pair * 16 + 16] = tile[:, 128:256].reshape(8, 1, 32, 128)
 
 
 def combine_kernel(slot_ref, weight_ref, rows_ref, out_ref, sum_ref):
@@ -421,15 +477,24 @@
 WHOLE = pl.BlockSpec(memory_space=pltpu.VMEM)
 
 
-def pack(query, key, value, decay, strength):
+def in_hbm(x):
+    return pltpu.with_memory_space_constraint(x, pltpu.HBM)
+
+
+def pack(half, query, key, value, decay, strength):
     return pl.pallas_call(
         pack_kernel,
         out_shape=shape((VALUE_HEADS, PACK_ROWS, 128), BF16),
-        in_specs=[WHOLE] * 5,
+        in_specs=[SMEM] + [pl.BlockSpec(memory_space=pltpu.HBM)] * 5,
         out_specs=WHOLE,
+        scratch_shapes=[
+            pltpu.VMEM((VALUE_HEADS, TOK), BF16),
+            pltpu.VMEM((VALUE_HEADS, TOK), BF16),
+            pltpu.SemaphoreType.DMA((4, VALUE_HEADS)),
+        ],
         compiler_params=params(),
         name="pack",
-    )(query, key, value, decay, strength)
+    )(half, *(in_hbm(x) for x in (query, key, value, decay, strength)))
 
 
 def route(ids, weights):
@@ -447,17 +512,17 @@
     )(ids, weights)
 
 
-def mixer(received):
+def mixer(received, weights):
     return pl.pallas_call(
         mixer_kernel,
         out_shape=(
             shape((BLOCKS, BLOCK, DH), BF16),
-            shape((BLOCKS, BLOCK, DH), F32),
-            shape((CHUNKS, MAP_ROWS, DH), F32),
+            pltpu.HBM((BLOCKS, BLOCK, DH), F32),
+            pltpu.HBM((CHUNKS, MAP_ROWS, DH), F32),
             shape((CHUNKS, 8, DH), F32),
             shape((HALF_ROWS, DH), BF16),
         ),
-        in_specs=[WHOLE],
+        in_specs=[WHOLE] + [pl.BlockSpec(memory_space=pl.ANY)] * 3,
         out_specs=(WHOLE,) * 5,
         scratch_shapes=[
             pltpu.VMEM((BLOCKS, BLOCK, DH), BF16),
@@ -467,7 +532,7 @@
         ],
         compiler_params=params(),
         name="mixer",
-    )(received)
+    )(received, *(in_hbm(w) for w in weights))
 
 
 def compose(half, own, other):
@@ -501,39 +566,39 @@
         scratch_shapes=[pltpu.VMEM((DH, DH), F32)],
         compiler_params=params(),
         name="heads",
-    )(half, own, other, other_map, query_part, local, sub_map, sub_gain)
-
-
-def mix(tok, heads, residual, out_gain, ffn_gain):
+    )(half, own, other, other_map, query_part, in_hbm(local), in_hbm(sub_map), sub_gain)
+
+
+def mix(half, tok, heads, residual, out_gain, ffn_gain):
     return pl.pallas_call(
         mixed_kernel,
         out_shape=(shape((TOK, D), BF16), shape((SLOTS, 16, 128), BF16)),
-        in_specs=[SMEM] + [WHOLE] * 4,
+        in_specs=[SMEM, SMEM] + [WHOLE] * 4,
         out_specs=(WHOLE, WHOLE),
         scratch_shapes=[pltpu.VMEM((TOK, 16, 128), BF16)],
         compiler_params=params(),
         name="mix",
-    )(tok, heads, residual, out_gain, ffn_gain)
-
-
-def experts(rows, gate, up, down):
-    hidden = gate.shape[1]
-    block = pl.BlockSpec((FFN_ROWS * 16, 128), lambda i: (i, 0))
+    )(half, tok, heads, residual, out_gain, ffn_gain)
+
+
+def experts(core, rows, weights):
+    def place(which, step, core_ref):
+        return (step, lax.rem(core_ref[0] + which, 2), 0, 0)
+
+    block = pl.BlockSpec((FFN_ROWS // 2, 1, 32, 128), place)
     return pl.pallas_call(
         expert_kernel,
-        grid=(SLOTS // FFN_ROWS,),
-        out_shape=shape((SLOTS * 16, 128), BF16),
-        in_specs=[
-            block,
-            pl.BlockSpec((D, hidden), lambda i: (0, 0)),
-            pl.BlockSpec((D, hidden), lambda i: (0, 0)),
-            pl.BlockSpec((hidden, D), lambda i: (0, 0)),
-        ],
-        out_specs=block,
-        scratch_shapes=[pltpu.VMEM((FFN_ROWS, D), BF16)],
+        grid_spec=pltpu.PrefetchScalarGridSpec(
+            num_scalar_prefetch=1,
+            grid=(2, EXPERTS // FFN_ROWS),
+            in_specs=[block] + [pl.BlockSpec(w.shape, lambda *_: (0, 0)) for w in weights],
+            out_specs=block,
+            scratch_shapes=[pltpu.VMEM((FFN_ROWS, D), BF16)],
+        ),
+        out_shape=shape((CHIPS, 2, 32, 128), BF16),
         compiler_params=params(),
         name="experts",
-    )(rows, gate, up, down)
+    )(core, rows, *weights)
 
 
 def combine(slots, weights, rows):
@@ -553,12 +618,17 @@
 
 
 def trade(x):
-    return lax.ppermute(x, "half", [(0, 1), (1, 0)])
+    return lax.ppermute(x, ("half", "pair"), [(0, 3), (3, 0), (1, 2), (2, 1)])
+
+
+def neighbour(x):
+    return lax.ppermute(x, "core", [(0, 1), (1, 0)])
 
 
 HEAD_AXES = ("pair", "y")
 SEQ_AXES = ("half", "pair", "y")
 EXP_AXES = ("z", "core")
+CHIP_AXES = SEQ_AXES + ("z",)
 
 
 def body(
@@ -576,12 +646,15 @@
     up_proj,
     down_proj,
 ):
-    sent = pack(mixer_query[0], mixer_key[0], mixer_value[0], log_decay[0].T, strength[0].T)
+    half = lax.axis_index("half").astype(jnp.int32).reshape(1)
+    core = lax.axis_index("core").astype(jnp.int32).reshape(1)
+    position = lax.axis_index(EXP_AXES).astype(jnp.int32).reshape(1)
+    sent = pack(half, mixer_query[0], mixer_key[0], mixer_value[0], log_decay[0].T, strength[0].T)
     received = swap_all(sent, HEAD_AXES)
     tok, slots, weights = route(expert_ids[0], expert_weights[0])
-    half = lax.axis_index("half").astype(jnp.int32).reshape(1)
-    position = lax.axis_index(EXP_AXES).astype(jnp.int32).reshape(1)
-    query_part, local, sub_map, sub_gain, own_map = mixer(received)
+    own = (gate_proj[0], up_proj[0], down_proj[0])
+    other = tuple(neighbour(w) for w in own)
+    query_part, local, sub_map, sub_gain, own_map = mixer(received, other)
     other_map = trade(own_map)
     maps = lax.all_gather(compose(half, own_map, other_map), EXP_AXES, axis=0)
     own_state = fold(position, maps)
@@ -589,11 +662,11 @@
     outs = head_rows(half, own_state, other_state, other_map, query_part, local, sub_map, sub_gain)
     heads = swap_all(outs, HEAD_AXES)
     mixed, outgoing = mix(
-        tok, heads, residual[0], out_gain.reshape(1, DH), ffn_gain.reshape(1, D)
+        half, tok, heads, residual[0], out_gain.reshape(1, DH), ffn_gain.reshape(1, D)
     )
-    arrived = swap_all(outgoing, SEQ_AXES + EXP_AXES)
-    result = experts(arrived.reshape(SLOTS * 16, 128), gate_proj[0], up_proj[0], down_proj[0])
-    returned = swap_all(result.reshape(SLOTS, 16, 128), SEQ_AXES + EXP_AXES)
+    arrived = swap_all(outgoing, CHIP_AXES)
+    result = experts(core, arrived.reshape(CHIPS, 2, 32, 128), own + other)
+    returned = swap_all(result.reshape(SLOTS, 16, 128), CHIP_AXES)
     ffn_out = combine(slots, weights, returned)
     return (mixed[None], ffn_out[None])
 

time: 335 us -> 342 us (1.021)
  blocking collectives: 279 us -> 254 us
  starting transfers between devices: 13.2 us -> 29.5 us
  waiting for transfers between devices: 9.64 us -> 19.9 us
  Pallas kernels: 27.4 us -> 34.5 us
    all_to_all x3 -> x2, blocking collectives: 250 us -> 223 us  [swap_all(): return lax.all_to_all(x, axes, split_axis=0, concat_axis=0, tiled=True)]
    ppermute x2 -> x5, starting transfers between devices: 8.73 us -> 17.2 us  [the longest x3 8.79 us: neighbour(): return lax.ppermute(x, 'core', [(0, 1), (1, 0)])]
    all_to_all x1 -> x2, starting transfers between devices: 4.42 us -> 12.3 us  [swap_all(): return lax.all_to_all(x, axes, split_axis=0, concat_axis=0, tiled=True)]
    all_to_all x1 -> x2, waiting for transfers between devices: 5.63 us -> 13.5 us  [swap_all(): return lax.all_to_all(x, axes, split_axis=0, concat_axis=0, tiled=True)]
  transfers between devices with their start and end apart: 3 -> 7, of which waited for: 3 -> 6; matrix products, arithmetic and copies ran while one was open for 0% -> 0% of each run, Pallas kernels for 1% -> 1%
where the time goes in v3:
time: 342 us; the launch traced here: 340 us
  blocking collectives  254 us (74%)
  Pallas kernels  34.5 us (10%)
  starting transfers between devices  29.5 us (9%)
  waiting for transfers between devices  19.9 us (6%)
    all_to_all x2, blocking collectives, swap_all(): return lax.all_to_all(x, axes, split_axis=0, concat_axis=0, tiled=True)  223 us
    all_gather x1, blocking collectives, body(): maps = lax.all_gather(compose(half, own_map, other_map), EXP_AXES, axis=0)  30.9 us
    all_to_all x2, waiting for transfers between devices, swap_all(): return lax.all_to_all(x, axes, split_axis=0, concat_axis=0, tiled=True)  13.5 us
    all_to_all x2, starting transfers between devices, swap_all(): return lax.all_to_all(x, axes, split_axis=0, concat_axis=0, tiled=True)  12.3 us
    pallas_call x1, Pallas kernels, mixer(): pl.pallas_call(mixer_kernel, out_shape=(shape((BLOCKS, BLOCK, DH), BF16),...  10.4 us
    pallas_call x1, Pallas kernels, experts(): pl.pallas_call(expert_kernel, grid_spec=pltpu.PrefetchScalarGridSpec(num_...  8.82 us
    ppermute x3, starting transfers between devices, neighbour(): return lax.ppermute(x, 'core', [(0, 1), (1, 0)])  8.79 us
    ppermute x2, starting transfers between devices, trade(): return lax.ppermute(x, ('half', 'pair'), [(0, 3), (3, 0), (1, 2), (2, 1)])  8.39 us
  transfers between devices with their start and end apart: 7, of which 6 were waited for; matrix products, arithmetic and copies ran while one was open for 0% of the time, Pallas kernels for 1%

profile of v3, /device:TPU:1, one launch (start us, length us, event | category | flops | bytes accessed | tf_op | source)
XLA Modules:
  0.0 340.3 jit_solution(3718938158703356075)
XLA Ops:
  0.6 2.6 pack.1
  3.2 8.7 %all-to-all-start = ((bf16[16,208,128]{2,1,0:T(8,128)(2,1)}), bf16[16,208,128]{2,1,0:T(8,128)(2,1)}, u32[]{:S(2)}, u32[]{:S(2)}) async-start(bf16[16,208,128]{2,1,0:T(8,128)(2,1)} %pack.1), calls=%async_computation | async-start | bytes 1703936 | tf_op jit(solution)/shard_map/all_to_all | solution.py:617
  12.0 4.3 %collective-permute-start = (bf16[2048,256]{1,0:T(8,128)(2,1)}, bf16[2048,256]{1,0:T(8,128)(2,1)S(1)}, u32[]{:S(2)}, u32[]{:S(2)}) collective-permute-start(bf16[2048,256]{1,0:T(8,128)(2,1)} %bitcast.28), channel_id=1, source_target_pairs={{0,1},{1,0},{2,3},{3,2},{4,5},{5,4},{6,7},{7,6},{8,9},{9,8},{10,11... | collective-permute-start | bytes 3145736 | tf_op jit(solution)/shard_map/ppermute | solution.py:625
  16.3 1.9 collective-permute-start.1
  18.2 0.0 copy-start.12
  18.3 0.0 copy-start.13
  18.3 0.0 copy-start.10
  18.3 0.0 copy-start.11
  18.3 2.5 collective-permute-start.2
  20.8 0.0 collective-permute-done.next_gate_ref.refs_3_
  20.9 0.0 copy-start
  20.9 0.2 collective-permute-done.1.next_up_ref.refs_4_
  21.1 0.0 copy-start.2
  21.1 2.2 collective-permute-done.2.next_down_ref.refs_5_
  23.3 0.0 copy-start.4
  23.3 7.9 %all-to-all-done.recv_ref = bf16[16,208,128]{2,1,0:T(8,128)(2,1)} async-done(((bf16[16,208,128]{2,1,0:T(8,128)(2,1)}), bf16[16,208,128]{2,1,0:T(8,128)(2,1)}, u32[]{:S(2)}, u32[]{:S(2)}) %all-to-all-start) | async-done | bytes 852000 | tf_op jit(solution)/shard_map/all_to_all | solution.py:617
  31.2 0.0 copy-done
  31.2 0.0 copy-done.2
  31.2 0.0 copy-done.4
  31.2 10.4 %mixer.1 = (bf16[16,64,128]{2,1,0:T(8,128)(2,1)S(1)}, f32[16,64,128]{2,1,0:T(8,128)}, f32[4,256,128]{2,1,0:T(8,128)}, f32[4,8,128]{2,1,0:T(8,128)S(1)}, bf16[288,128]{1,0:T(8,128)(2,1)S(1)}) custom-call(bf16[16,208,128]{2,1,0:T(8,128)(2,1)} %all-to-all-done.recv_ref, bf16[2048,256]{1,0:T(8,128)(2,1)} %copy-done, bf16[2048,256]{1,0:T(8,128)(2,1)} %copy-done.2, ...), custom_call_target="tpu_custom_call" | custom-call | tf_op jit(solution)/shard_map/mixer/pallas_call | solution.py:516
  41.6 4.7 %collective-permute-start.3 = (bf16[288,128]{1,0:T(8,128)(2,1)S(1)}, bf16[288,128]{1,0:T(8,128)(2,1)S(1)}, u32[]{:S(2)}, u32[]{:S(2)}) collective-permute-start(bf16[288,128]{1,0:T(8,128)(2,1)S(1)} %get-tuple-element.13.own_ref), channel_id=1, source_target_pairs={{0,384},{384,0},{128,256},{256,128},{1,385},{385,1},{129,257},{257... | collective-permute-start | bytes 221192 | tf_op jit(solution)/shard_map/ppermute | solution.py:621
  46.3 1.7 collective-permute-done.3.other_ref.other_map_ref
  48.1 0.2 compose.1
  48.2 30.9 %all-gather = bf16[3584,128]{1,0:T(8,128)(2,1)S(1)} all-gather(bf16[224,128]{1,0:T(8,128)(2,1)S(1)} %compose.1), channel_id=2, replica_groups=mesh['half'=2,'pair'=2,'y'=8,'z'=8,'core'=2] {'z','core'}, dimensions={0}, use_global_device_ids=true | all-gather | bytes 974848 | tf_op jit(solution)/shard_map/all_gather | solution.py:659
  79.1 0.1 fold.1.own_ref
  79.3 3.6 %collective-permute-start.4 = (f32[64,128]{1,0:T(8,128)S(1)}, f32[64,128]{1,0:T(8,128)S(1)}, u32[]{:S(2)}, u32[]{:S(2)}) collective-permute-start(f32[64,128]{1,0:T(8,128)S(1)} %fold.1.own_ref), channel_id=1, source_target_pairs={{0,384},{384,0},{128,256},{256,128},{1,385},{385,1},{129,257},{257... | collective-permute-start | bytes 98312 | tf_op jit(solution)/shard_map/ppermute | solution.py:621
  82.9 2.2 collective-permute-done.4.other_ref
  85.1 2.7 heads.1
  87.9 3.6 %all-to-all-start.1 = ((bf16[16,64,128]{2,1,0:T(8,128)(2,1)}), bf16[16,64,128]{2,1,0:T(8,128)(2,1)S(1)}, u32[]{:S(2)}, u32[]{:S(2)}) async-start(bf16[16,64,128]{2,1,0:T(8,128)(2,1)} %heads.1), calls=%async_computation.1 | async-start | bytes 524288 | tf_op jit(solution)/shard_map/all_to_all | solution.py:617
  91.4 0.0 copy-done.12
  91.4 0.1 copy.15
  91.5 0.0 copy-done.13
  91.5 0.1 copy.16
  91.6 2.1 route.1
  93.7 5.6 %all-to-all-done.1.heads_ref = bf16[16,64,128]{2,1,0:T(8,128)(2,1)S(1)} async-done(((bf16[16,64,128]{2,1,0:T(8,128)(2,1)}), bf16[16,64,128]{2,1,0:T(8,128)(2,1)S(1)}, u32[]{:S(2)}, u32[]{:S(2)}) %all-to-all-start.1) | async-done | bytes 262176 | tf_op jit(solution)/shard_map/all_to_all | solution.py:617
  99.3 0.0 copy-done.10
  99.3 0.0 copy-done.11
  99.4 0.0 copy-start.9
  99.4 0.9 copy-done.9
  100.3 3.9 %mix.1 = (bf16[64,2048]{1,0:T(8,128)(2,1)}, bf16[1024,16,128]{2,1,0:T(8,128)(2,1)S(1)}) custom-call(s32[1]{0:T(128)} %bitcast.half_ref, s32[2,512]{1,0:T(2,128)S(1)} %get-tuple-element.12.tok_ref, bf16[16,64,128]{2,1,0:T(8,128)(2,1)S(1)} %all-to-all-done.1.heads_ref, bf16[64,2048]{1,0:T(8,128)(2,1)S(1)} %bitcast.34, f32[1,128]{1,0:T(1,128)S(1)} %bitcast.38, ...), custom_call_target="tpu_custom_call" | custom-call | tf_op jit(solution)/shard_map/mix/pallas_call | solution.py:573
  104.2 0.0 copy-start.1
  104.2 0.0 copy-start.3
  104.2 0.0 copy-start.5
  104.2 0.0 copy-start.6
  104.2 0.0 copy-start.7
  104.2 0.0 copy-start.8
  104.2 111.3 %all_to_all.20 = bf16[1024,16,128]{2,1,0:T(8,128)(2,1)S(1)} all-to-all(bf16[1024,16,128]{2,1,0:T(8,128)(2,1)S(1)} %get-tuple-element.21), channel_id=1, replica_groups=mesh['half'=2,'pair'=2,'y'=8,'z'=8,'core'=2] {'half','pair','y','z'}, dimensions={0} | all-to-all | bytes 8388608 | tf_op jit(solution)/shard_map/all_to_all | solution.py:617
  215.6 0.0 copy-done.1
  215.6 0.0 copy-done.3
  215.6 0.0 copy-done.5
  215.6 0.0 copy-done.6
  215.6 0.0 copy-done.7
  215.6 0.0 copy-done.8
  215.6 8.8 %experts.1 = bf16[256,2,32,128]{3,2,1,0:T(8,128)(2,1)S(1)} custom-call(s32[1]{0:T(128)} %bitcast.19.core_ref, bf16[256,2,32,128]{3,2,1,0:T(8,128)(2,1)S(1)} %bitcast.25, bf16[2048,256]{1,0:T(8,128)(2,1)S(1)} %bitcast.29, bf16[2048,256]{1,0:T(8,128)(2,1)S(1)} %bitcast.31, bf16[256,2048]{1,0:T(8,128)(2,1)S(1)} %bitcast.33, bf16[2048,256]{1,0:T(8,128)(2,1)S(1)} %copy-done.1, ...), custom_call_target="tpu_custom_call" | custom-call | tf_op jit(solution)/shard_map/experts/pallas_call | solution.py:589
  224.4 112.1 %all_to_all.21.rows_ref = bf16[1024,16,128]{2,1,0:T(8,128)(2,1)S(1)} all-to-all(bf16[1024,16,128]{2,1,0:T(8,128)(2,1)S(1)} %bitcast.26), channel_id=1, replica_groups=mesh['half'=2,'pair'=2,'y'=8,'z'=8,'core'=2] {'half','pair','y','z'}, dimensions={0} | all-to-all | bytes 8388608 | tf_op jit(solution)/shard_map/all_to_all | solution.py:617
  336.6 3.7 %combine.1 = bf16[64,2048]{1,0:T(8,128)(2,1)} custom-call(s32[64,128]{1,0:T(8,128)S(1)} %get-tuple-element.19.slot_ref, f32[64,128]{1,0:T(8,128)S(1)} %get-tuple-element.20.weight_ref, bf16[1024,16,128]{2,1,0:T(8,128)(2,1)S(1)} %all_to_all.21.rows_ref), custom_call_target="tpu_custom_call" | custom-call | tf_op jit(solution)/shard_map/combine/pallas_call | solution.py:605
Async XLA Ops:
  3.2 27.9 %all-to-all-start = ((bf16[16,208,128]{2,1,0:T(8,128)(2,1)}), bf16[16,208,128]{2,1,0:T(8,128)(2,1)}, u32[]{:S(2)}, u32[]{:S(2)}) async-start(bf16[16,208,128]{2,1,0:T(8,128)(2,1)} %pack.1), calls=%async_computation | async-start | bytes 1703936 | tf_op jit(solution)/shard_map/all_to_all | solution.py:617
  12.0 8.9 %collective-permute-start = (bf16[2048,256]{1,0:T(8,128)(2,1)}, bf16[2048,256]{1,0:T(8,128)(2,1)S(1)}, u32[]{:S(2)}, u32[]{:S(2)}) collective-permute-start(bf16[2048,256]{1,0:T(8,128)(2,1)} %bitcast.28), channel_id=1, source_target_pairs={{0,1},{1,0},{2,3},{3,2},{4,5},{5,4},{6,7},{7,6},{8,9},{9,8},{10,11... | collective-permute-start | bytes 3145736 | tf_op jit(solution)/shard_map/ppermute | solution.py:625
  16.3 4.8 %collective-permute-start.1 = (bf16[2048,256]{1,0:T(8,128)(2,1)}, bf16[2048,256]{1,0:T(8,128)(2,1)S(1)}, u32[]{:S(2)}, u32[]{:S(2)}) collective-permute-start(bf16[2048,256]{1,0:T(8,128)(2,1)} %bitcast.30), channel_id=1, source_target_pairs={{0,1},{1,0},{2,3},{3,2},{4,5},{5,4},{6,7},{7,6},{8,9},{9,8},{10,11... | collective-permute-start | bytes 3145736 | tf_op jit(solution)/shard_map/ppermute | solution.py:625
  18.2 73.2 %copy-start.12 = (s32[1,64,10]{1,0,2:T(1,128)S(1)}, s32[1,64,10]{1,0,2:T(1,128)}, u32[]{:S(2)}) copy-start(s32[1,64,10]{1,0,2:T(1,128)} %param.21) | copy-start | bytes 7684
  18.3 73.3 %copy-start.13 = (f32[1,64,10]{1,0,2:T(1,128)S(1)}, f32[1,64,10]{1,0,2:T(1,128)}, u32[]{:S(2)}) copy-start(f32[1,64,10]{1,0,2:T(1,128)} %param.22) | copy-start | bytes 7684
  18.3 81.1 %copy-start.10 = (f32[2048]{0:T(1024)S(1)}, f32[2048]{0:T(1024)}, u32[]{:S(2)}) copy-start(f32[2048]{0:T(1024)} %param.20) | copy-start | bytes 24580
  18.3 81.1 %copy-start.11 = (f32[128]{0:T(128)S(1)}, f32[128]{0:T(128)}, u32[]{:S(2)}) copy-start(f32[128]{0:T(128)} %param.19) | copy-start | bytes 1540
  18.3 5.0 %collective-permute-start.2 = (bf16[256,2048]{1,0:T(8,128)(2,1)}, bf16[256,2048]{1,0:T(8,128)(2,1)S(1)}, u32[]{:S(2)}, u32[]{:S(2)}) collective-permute-start(bf16[256,2048]{1,0:T(8,128)(2,1)} %bitcast.32), channel_id=1, source_target_pairs={{0,1},{1,0},{2,3},{3,2},{4,5},{5,4},{6,7},{7,6},{8,9},{9,8},{10,11... | collective-permute-start | bytes 3145736 | tf_op jit(solution)/shard_map/ppermute | solution.py:625
  20.9 10.3 %copy-start = (bf16[2048,256]{1,0:T(8,128)(2,1)}, bf16[2048,256]{1,0:T(8,128)(2,1)S(1)}, u32[]{:S(2)}) copy-start(bf16[2048,256]{1,0:T(8,128)(2,1)S(1)} %collective-permute-done.next_gate_ref.refs_3_) | copy-start | bytes 3145732
  21.1 10.1 %copy-start.2 = (bf16[2048,256]{1,0:T(8,128)(2,1)}, bf16[2048,256]{1,0:T(8,128)(2,1)S(1)}, u32[]{:S(2)}) copy-start(bf16[2048,256]{1,0:T(8,128)(2,1)S(1)} %collective-permute-done.1.next_up_ref.refs_4_) | copy-start | bytes 3145732
  23.3 7.9 %copy-start.4 = (bf16[256,2048]{1,0:T(8,128)(2,1)}, bf16[256,2048]{1,0:T(8,128)(2,1)S(1)}, u32[]{:S(2)}) copy-start(bf16[256,2048]{1,0:T(8,128)(2,1)S(1)} %collective-permute-done.2.next_down_ref.refs_5_) | copy-start | bytes 3145732
  41.6 6.5 %collective-permute-start.3 = (bf16[288,128]{1,0:T(8,128)(2,1)S(1)}, bf16[288,128]{1,0:T(8,128)(2,1)S(1)}, u32[]{:S(2)}, u32[]{:S(2)}) collective-permute-start(bf16[288,128]{1,0:T(8,128)(2,1)S(1)} %get-tuple-element.13.own_ref), channel_id=1, source_target_pairs={{0,384},{384,0},{128,256},{256,128},{1,385},{385,1},{129,257},{257... | collective-permute-start | bytes 221192 | tf_op jit(solution)/shard_map/ppermute | solution.py:621
  79.3 5.9 %collective-permute-start.4 = (f32[64,128]{1,0:T(8,128)S(1)}, f32[64,128]{1,0:T(8,128)S(1)}, u32[]{:S(2)}, u32[]{:S(2)}) collective-permute-start(f32[64,128]{1,0:T(8,128)S(1)} %fold.1.own_ref), channel_id=1, source_target_pairs={{0,384},{384,0},{128,256},{256,128},{1,385},{385,1},{129,257},{257... | collective-permute-start | bytes 98312 | tf_op jit(solution)/shard_map/ppermute | solution.py:621
  87.9 11.5 %all-to-all-start.1 = ((bf16[16,64,128]{2,1,0:T(8,128)(2,1)}), bf16[16,64,128]{2,1,0:T(8,128)(2,1)S(1)}, u32[]{:S(2)}, u32[]{:S(2)}) async-start(bf16[16,64,128]{2,1,0:T(8,128)(2,1)} %heads.1), calls=%async_computation.1 | async-start | bytes 524288 | tf_op jit(solution)/shard_map/all_to_all | solution.py:617
  99.4 1.0 copy-start.9
  104.2 111.3 %copy-start.1 = (bf16[2048,256]{1,0:T(8,128)(2,1)S(1)}, bf16[2048,256]{1,0:T(8,128)(2,1)}, u32[]{:S(2)}) copy-start(bf16[2048,256]{1,0:T(8,128)(2,1)} %copy-done) | copy-start | bytes 3145732
  104.2 111.3 %copy-start.3 = (bf16[2048,256]{1,0:T(8,128)(2,1)S(1)}, bf16[2048,256]{1,0:T(8,128)(2,1)}, u32[]{:S(2)}) copy-start(bf16[2048,256]{1,0:T(8,128)(2,1)} %copy-done.2) | copy-start | bytes 3145732
  104.2 111.3 %copy-start.5 = (bf16[256,2048]{1,0:T(8,128)(2,1)S(1)}, bf16[256,2048]{1,0:T(8,128)(2,1)}, u32[]{:S(2)}) copy-start(bf16[256,2048]{1,0:T(8,128)(2,1)} %copy-done.4) | copy-start | bytes 3145732
  104.2 111.3 %copy-start.6 = (bf16[1,2048,256]{2,1,0:T(8,128)(2,1)S(1)}, bf16[1,2048,256]{2,1,0:T(8,128)(2,1)}, u32[]{:S(2)}) copy-start(bf16[1,2048,256]{2,1,0:T(8,128)(2,1)} %param.23) | copy-start | bytes 3145732
  104.2 111.3 %copy-start.7 = (bf16[1,2048,256]{2,1,0:T(8,128)(2,1)S(1)}, bf16[1,2048,256]{2,1,0:T(8,128)(2,1)}, u32[]{:S(2)}) copy-start(bf16[1,2048,256]{2,1,0:T(8,128)(2,1)} %param.24) | copy-start | bytes 3145732
  104.2 111.3 %copy-start.8 = (bf16[1,256,2048]{2,1,0:T(8,128)(2,1)S(1)}, bf16[1,256,2048]{2,1,0:T(8,128)(2,1)}, u32[]{:S(2)}) copy-start(bf16[1,256,2048]{2,1,0:T(8,128)(2,1)} %param.25) | copy-start | bytes 3145732

commit v4 on v2

--- a/solution.py
+++ b/solution.py
@@ -16,7 +16,7 @@
 EXPERTS = 512
 WIDTH = 64
 BLOCKS = 16
-GROUP = 8
+GROUP = 16
 CHUNKS = 4
 STEPS = 4
 PACK_ROWS = 3 * TOK + 16
@@ -59,26 +59,51 @@
     return high, (x - high.astype(F32)).astype(BF16)
 
 
-def bdot3(a, b):
-    ah, al = split(a)
-    bh, bl = split(b)
-    return bdot_nn(ah, bh) + (bdot_nn(ah, bl) + bdot_nn(al, bh))
-
-
 def swap_matrix():
     out_index = lax.broadcasted_iota(jnp.int32, (256, 256), 0)
     in_index = lax.broadcasted_iota(jnp.int32, (256, 256), 1)
     return (in_index == (out_index % 16) * 16 + out_index // 16).astype(BF16)
 
 
-def pack_kernel(query_ref, key_ref, value_ref, decay_ref, strength_ref, out_ref):
-    gates = jnp.concatenate([decay_ref[...].astype(F32), strength_ref[...].astype(F32)], axis=1)
+def pack_kernel(
+    half_ref,
+    query_ref,
+    key_ref,
+    value_ref,
+    decay_ref,
+    strength_ref,
+    out_ref,
+    decay_rows,
+    strength_rows,
+    sems,
+):
+    gate_copies = [
+        pltpu.make_async_copy(decay_ref, decay_rows, sems.at[3, 0]),
+        pltpu.make_async_copy(strength_ref, strength_rows, sems.at[3, 1]),
+    ]
+    copies = []
     for head in range(VALUE_HEADS):
-        shared = slice(head // 2 * DH, head // 2 * DH + DH)
-        out_ref[head, 0:64, :] = query_ref[:, shared]
-        out_ref[head, 64:128, :] = key_ref[:, shared]
-        out_ref[head, 128:192, :] = value_ref[:, head * DH : head * DH + DH]
-        out_ref[head, 192:208, :] = jnp.broadcast_to(gates[head : head + 1], (16, 128)).astype(BF16)
+        place = lax.rem(head + half_ref[0] * 8, VALUE_HEADS)
+        for part, (ref, column) in enumerate(
+            ((query_ref, head // 2), (key_ref, head // 2), (value_ref, head))
+        ):
+            copies.append(
+                pltpu.make_async_copy(
+                    ref.at[:, column * DH : column * DH + DH],
+                    out_ref.at[place, part * TOK : part * TOK + TOK, :],
+                    sems.at[part, head],
+                )
+            )
+    for copy in gate_copies + copies:
+        copy.start()
+    for copy in gate_copies:
+        copy.wait()
+    gates = jnp.concatenate([decay_rows[...].astype(F32), strength_rows[...].astype(F32)], axis=1)
+    for head in range(VALUE_HEADS):
+        place = lax.rem(head + half_ref[0] * 8, VALUE_HEADS)
+        out_ref[place, 192:208, :] = jnp.broadcast_to(gates[head : head + 1], (16, 128)).astype(BF16)
+    for copy in copies:
+        copy.wait()
 
 
 def route_kernel(ids_ref, weight_in_ref, tok_ref, slot_ref, weight_ref):
@@ -101,8 +126,10 @@
         mine = jnp.sum(jnp.where(ids == expert, rank, 0.0), axis=1, keepdims=True)
         slots = jnp.where(lane == k, 2 * ids + mine.astype(jnp.int32), slots)
         weights = jnp.where(lane == k, weight_in_ref[:, k : k + 1], weights)
-    slot_ref[...] = slots
-    weight_ref[...] = weights
+    slot_ref[:, 0:TOK] = jnp.transpose(slots.astype(F32))[0:16].astype(jnp.int32)
+    slot_ref[:, TOK:128] = jnp.zeros((16, 128 - TOK), jnp.int32)
+    weight_ref[:, 0:TOK] = jnp.transpose(weights)[0:16]
+    weight_ref[:, TOK:128] = jnp.zeros((16, 128 - TOK), F32)
 
 
 def spread_gain(gain):
@@ -168,13 +195,8 @@
         key_dot = bdot_nt(k, k) * (k_norm * k_norm_row)
         query_dot = bdot_nt(q, k) * (q_norm * k_norm_row)
         negated = jnp.where(lower, -(strength * key_dot * fade), 0.0)
-        base = jnp.where(same(8), negated, 0.0)
-        inverse = identity + base
-        powered = bdot3(base, base)
-        inverse = inverse + bdot3(inverse, powered)
-        powered = bdot3(powered, powered)
-        inverse = inverse + bdot3(inverse, powered)
-        for size in (8, 16, 32):
+        inverse = identity + jnp.where(same(2), negated, 0.0)
+        for size in (2, 4, 8, 16, 32):
             cross = jnp.where(same(2 * size) & ~same(size), negated, 0.0).astype(BF16)
             half = inverse.astype(BF16)
             inverse = inverse + bdot_nn(bdot_nn(half, cross).astype(BF16), half)
@@ -336,12 +358,20 @@
 
 
 def mixed_kernel(
-    tok_ref, heads_ref, residual_ref, out_gain_ref, ffn_gain_ref, mixed_ref, send_ref, rows_ref
+    half_ref,
+    tok_ref,
+    heads_ref,
+    residual_ref,
+    out_gain_ref,
+    ffn_gain_ref,
+    mixed_ref,
+    send_ref,
+    rows_ref,
 ):
     gain = out_gain_ref[...]
     total = jnp.zeros((TOK, 1), F32)
     for head in range(VALUE_HEADS):
-        wide = heads_ref[head].astype(F32)
+        wide = heads_ref[lax.rem(head + half_ref[0] * 8, VALUE_HEADS)].astype(F32)
         scale = lax.rsqrt(jnp.mean(wide * wide, axis=1, keepdims=True) + 1e-06)
         part = slice(head * DH, head * DH + DH)
         mixed = (residual_ref[:, part].astype(F32) + wide * scale * gain).astype(BF16)
@@ -361,8 +391,8 @@
         rows_ref[tokens] = swapped.reshape(16, 16, 128)
 
     def place(expert, unused):
-        send_ref[2 * expert] = rows_ref[tok_ref[0, expert]]
-        send_ref[2 * expert + 1] = rows_ref[tok_ref[1, expert]]
+        send_ref[2 * expert] = rows_ref[tok_ref[expert]]
+        send_ref[2 * expert + 1] = rows_ref[tok_ref[EXPERTS + expert]]
         return unused
 
     lax.fori_loop(0, EXPERTS, place, 0, unroll=16)
@@ -400,11 +430,12 @@
     def token(index, unused):
         total = jnp.zeros((16, 128), F32)
         for k in range(TOPK):
-            total = total + weight_ref[index, k] * rows_ref[slot_ref[index, k]].astype(F32)
+            place = k * 128 + index
+            total = total + weight_ref[place] * rows_ref[slot_ref[place]].astype(F32)
         sum_ref[index] = total.astype(BF16)
         return unused
 
-    lax.fori_loop(0, TOK, token, 0, unroll=2)
+    lax.fori_loop(0, TOK, token, 0, unroll=4)
     swap = swap_matrix()
     for group in range(TOK // 16):
         tokens = slice(group * 16, group * 16 + 16)
@@ -421,15 +452,24 @@
 WHOLE = pl.BlockSpec(memory_space=pltpu.VMEM)
 
 
-def pack(query, key, value, decay, strength):
+def in_hbm(x):
+    return pltpu.with_memory_space_constraint(x, pltpu.HBM)
+
+
+def pack(half, query, key, value, decay, strength):
     return pl.pallas_call(
         pack_kernel,
         out_shape=shape((VALUE_HEADS, PACK_ROWS, 128), BF16),
-        in_specs=[WHOLE] * 5,
+        in_specs=[SMEM] + [pl.BlockSpec(memory_space=pltpu.HBM)] * 5,
         out_specs=WHOLE,
+        scratch_shapes=[
+            pltpu.VMEM((VALUE_HEADS, TOK), BF16),
+            pltpu.VMEM((VALUE_HEADS, TOK), BF16),
+            pltpu.SemaphoreType.DMA((4, VALUE_HEADS)),
+        ],
         compiler_params=params(),
         name="pack",
-    )(query, key, value, decay, strength)
+    )(half, *(in_hbm(x) for x in (query, key, value, decay, strength)))
 
 
 def route(ids, weights):
@@ -437,8 +477,8 @@
         route_kernel,
         out_shape=(
             shape((2, EXPERTS), jnp.int32),
-            shape((TOK, 128), jnp.int32),
-            shape((TOK, 128), F32),
+            shape((16, 128), jnp.int32),
+            shape((16, 128), F32),
         ),
         in_specs=[WHOLE, WHOLE],
         out_specs=(WHOLE, WHOLE, WHOLE),
@@ -504,16 +544,16 @@
     )(half, own, other, other_map, query_part, local, sub_map, sub_gain)
 
 
-def mix(tok, heads, residual, out_gain, ffn_gain):
+def mix(half, tok, heads, residual, out_gain, ffn_gain):
     return pl.pallas_call(
         mixed_kernel,
         out_shape=(shape((TOK, D), BF16), shape((SLOTS, 16, 128), BF16)),
-        in_specs=[SMEM] + [WHOLE] * 4,
+        in_specs=[SMEM, SMEM] + [WHOLE] * 4,
         out_specs=(WHOLE, WHOLE),
         scratch_shapes=[pltpu.VMEM((TOK, 16, 128), BF16)],
         compiler_params=params(),
         name="mix",
-    )(tok, heads, residual, out_gain, ffn_gain)
+    )(half, tok.reshape(SLOTS), heads, residual, out_gain, ffn_gain)
 
 
 def experts(rows, gate, up, down):
@@ -545,7 +585,7 @@
         scratch_shapes=[pltpu.VMEM((TOK, 16, 128), BF16)],
         compiler_params=params(),
         name="combine",
-    )(slots, weights, rows)
+    )(slots.reshape(16 * 128), weights.reshape(16 * 128), rows)
 
 
 def swap_all(x, axes):
@@ -553,7 +593,7 @@
 
 
 def trade(x):
-    return lax.ppermute(x, "half", [(0, 1), (1, 0)])
+    return lax.ppermute(x, ("half", "pair"), [(0, 3), (3, 0), (1, 2), (2, 1)])
 
 
 HEAD_AXES = ("pair", "y")
@@ -576,11 +616,11 @@
     up_proj,
     down_proj,
 ):
-    sent = pack(mixer_query[0], mixer_key[0], mixer_value[0], log_decay[0].T, strength[0].T)
+    half = lax.axis_index("half").astype(jnp.int32).reshape(1)
+    position = lax.axis_index(EXP_AXES).astype(jnp.int32).reshape(1)
+    sent = pack(half, mixer_query[0], mixer_key[0], mixer_value[0], log_decay[0].T, strength[0].T)
     received = swap_all(sent, HEAD_AXES)
     tok, slots, weights = route(expert_ids[0], expert_weights[0])
-    half = lax.axis_index("half").astype(jnp.int32).reshape(1)
-    position = lax.axis_index(EXP_AXES).astype(jnp.int32).reshape(1)
     query_part, local, sub_map, sub_gain, own_map = mixer(received)
     other_map = trade(own_map)
     maps = lax.all_gather(compose(half, own_map, other_map), EXP_AXES, axis=0)
@@ -589,7 +629,7 @@
     outs = head_rows(half, own_state, other_state, other_map, query_part, local, sub_map, sub_gain)
     heads = swap_all(outs, HEAD_AXES)
     mixed, outgoing = mix(
-        tok, heads, residual[0], out_gain.reshape(1, DH), ffn_gain.reshape(1, D)
+        half, tok, heads, residual[0], out_gain.reshape(1, DH), ffn_gain.reshape(1, D)
     )
     arrived = swap_all(outgoing, SEQ_AXES + EXP_AXES)
     result = experts(arrived.reshape(SLOTS * 16, 128), gate_proj[0], up_proj[0], down_proj[0])

time: 335 us -> 328 us (0.979)
  local copies, waits for them, and re-layouts: 4.35 us -> 0.22 us
    unnamed x28 -> x19, local copies, waits for them, and re-layouts: 4.35 us -> 0.22 us
where the time goes in v4:
time: 328 us
  blocking collectives  279 us (85%)
  Pallas kernels  25.1 us (8%)
  starting transfers between devices  11.8 us (4%)
  waiting for transfers between devices  10.2 us (3%)
    all_to_all x3, blocking collectives, swap_all(): return lax.all_to_all(x, axes, split_axis=0, concat_axis=0, tiled=True)  251 us
    all_gather x1, blocking collectives, body(): maps = lax.all_gather(compose(half, own_map, other_map), EXP_AXES, axis=0)  28.9 us
    ppermute x2, starting transfers between devices, trade(): return lax.ppermute(x, ('half', 'pair'), [(0, 3), (3, 0), (1, 2), (2, 1)])  7.54 us
    pallas_call x1, Pallas kernels, experts(): pl.pallas_call(expert_kernel, grid=(SLOTS // FFN_ROWS,), out_shape=shape(...  7.18 us
  transfers between devices with their start and end apart: 3, of which 3 were waited for; matrix products, arithmetic and copies ran while one was open for 0% of the time, Pallas kernels for 1%

profile of v4, /device:TPU:1, one launch (start us, length us, event | category | flops | bytes accessed | tf_op | source)
XLA Modules:
  0.0 327.5 jit_solution(2046457357501533518)
XLA Ops:
  0.6 0.0 copy-start.6
  0.6 0.0 copy-start.7
  0.7 0.0 copy-start.3
  0.7 0.0 copy-start.4
  0.7 0.0 copy-start.5
  0.7 1.7 pack.1
  2.4 29.8 %all_to_all.20.recv_ref = bf16[16,208,128]{2,1,0:T(8,128)(2,1)S(1)} all-to-all(bf16[16,208,128]{2,1,0:T(8,128)(2,1)S(1)} %pack.1), channel_id=1, replica_groups=mesh['half'=2,'pair'=2,'y'=8,'z'=8,'core'=2] {'pair','y'}, dimensions={0} | all-to-all | bytes 1703936 | tf_op jit(solution)/shard_map/all_to_all | solution.py:592
  32.2 6.3 %mixer.1 = (bf16[16,64,128]{2,1,0:T(8,128)(2,1)S(1)}, f32[16,64,128]{2,1,0:T(8,128)S(1)}, f32[4,256,128]{2,1,0:T(8,128)S(1)}, f32[4,8,128]{2,1,0:T(8,128)S(1)}, bf16[288,128]{1,0:T(8,128)(2,1)S(1)}) custom-call(bf16[16,208,128]{2,1,0:T(8,128)(2,1)S(1)} %all_to_all.20.recv_ref), custom_call_target="tpu_custom_call" | custom-call | tf_op jit(solution)/shard_map/mixer/pallas_call | solution.py:491
  38.5 3.4 %collective-permute-start = (bf16[288,128]{1,0:T(8,128)(2,1)S(1)}, bf16[288,128]{1,0:T(8,128)(2,1)S(1)}, u32[]{:S(2)}, u32[]{:S(2)}) collective-permute-start(bf16[288,128]{1,0:T(8,128)(2,1)S(1)} %get-tuple-element.13.own_ref), channel_id=1, source_target_pairs={{0,384},{384,0},{128,256},{256,128},{1,385},{385,1},{129,257},{257... | collective-permute-start | bytes 221192 | tf_op jit(solution)/shard_map/ppermute | solution.py:596
  41.8 2.9 collective-permute-done.other_ref.other_map_ref
  44.8 0.2 compose.1
  44.9 28.9 %all-gather = bf16[3584,128]{1,0:T(8,128)(2,1)S(1)} all-gather(bf16[224,128]{1,0:T(8,128)(2,1)S(1)} %compose.1), channel_id=2, replica_groups=mesh['half'=2,'pair'=2,'y'=8,'z'=8,'core'=2] {'z','core'}, dimensions={0}, use_global_device_ids=true | all-gather | bytes 974848 | tf_op jit(solution)/shard_map/all_gather | solution.py:626
  73.8 0.1 fold.1.own_ref
  74.0 4.2 %collective-permute-start.1 = (f32[64,128]{1,0:T(8,128)S(1)}, f32[64,128]{1,0:T(8,128)S(1)}, u32[]{:S(2)}, u32[]{:S(2)}) collective-permute-start(f32[64,128]{1,0:T(8,128)S(1)} %fold.1.own_ref), channel_id=1, source_target_pairs={{0,384},{384,0},{128,256},{256,128},{1,385},{385,1},{129,257},{257... | collective-permute-start | bytes 98312 | tf_op jit(solution)/shard_map/ppermute | solution.py:596
  78.2 1.7 collective-permute-done.1.other_ref
  79.8 1.5 heads.1
  81.4 4.2 %all-to-all-start.1 = ((bf16[16,64,128]{2,1,0:T(8,128)(2,1)}), bf16[16,64,128]{2,1,0:T(8,128)(2,1)S(1)}, u32[]{:S(2)}, u32[]{:S(2)}) async-start(bf16[16,64,128]{2,1,0:T(8,128)(2,1)} %heads.1), calls=%async_computation.1 | async-start | bytes 524288 | tf_op jit(solution)/shard_map/all_to_all | solution.py:592
  85.6 0.0 copy-done.6
  85.6 0.1 copy.15
  85.7 0.0 copy-done.7
  85.7 0.1 copy.16
  85.8 2.1 route.1
  87.9 5.6 %all-to-all-done.1.heads_ref = bf16[16,64,128]{2,1,0:T(8,128)(2,1)S(1)} async-done(((bf16[16,64,128]{2,1,0:T(8,128)(2,1)}), bf16[16,64,128]{2,1,0:T(8,128)(2,1)S(1)}, u32[]{:S(2)}, u32[]{:S(2)}) %all-to-all-start.1) | async-done | bytes 262176 | tf_op jit(solution)/shard_map/all_to_all | solution.py:592
  93.5 0.0 copy-done.3
  93.5 0.0 copy-done.4
  93.5 0.0 copy-done.5
  93.5 3.2 mix.1
  96.7 0.0 copy-start
  96.7 0.0 copy-start.1
  96.7 0.0 copy-start.2
  96.7 112.4 %all_to_all.21 = bf16[1024,16,128]{2,1,0:T(8,128)(2,1)S(1)} all-to-all(bf16[1024,16,128]{2,1,0:T(8,128)(2,1)S(1)} %get-tuple-element.21), channel_id=1, replica_groups=mesh['half'=2,'pair'=2,'y'=8,'z'=8,'core'=2] {'half','pair','y','z','core'}, dimensions={0} | all-to-all | bytes 8388608 | tf_op jit(solution)/shard_map/all_to_all | solution.py:592
  209.1 0.0 copy-done
  209.1 0.0 copy-done.1
  209.1 0.0 copy-done.2
  209.1 7.2 %experts.1 = bf16[16384,128]{1,0:T(8,128)(2,1)S(1)} custom-call(bf16[16384,128]{1,0:T(8,128)(2,1)S(1)} %bitcast.28, bf16[2048,256]{1,0:T(8,128)(2,1)S(1)} %bitcast.31, bf16[2048,256]{1,0:T(8,128)(2,1)S(1)} %bitcast.32, bf16[256,2048]{1,0:T(8,128)(2,1)S(1)} %bitcast.33), custom_call_target="tpu_custom_call" | custom-call | tf_op jit(solution)/shard_map/experts/pallas_call | solution.py:562
  216.3 108.4 %all_to_all.22.rows_ref = bf16[1024,16,128]{2,1,0:T(8,128)(2,1)S(1)} all-to-all(bf16[1024,16,128]{2,1,0:T(8,128)(2,1)S(1)} %bitcast.29), channel_id=1, replica_groups=mesh['half'=2,'pair'=2,'y'=8,'z'=8,'core'=2] {'half','pair','y','z','core'}, dimensions={0} | all-to-all | bytes 8388608 | tf_op jit(solution)/shard_map/all_to_all | solution.py:592
  324.7 2.8 combine.1
  (1 shorter events, 0.0 us)
Async XLA Ops:
  0.6 85.0 %copy-start.6 = (s32[1,64,10]{1,0,2:T(1,128)S(1)}, s32[1,64,10]{1,0,2:T(1,128)}, u32[]{:S(2)}) copy-start(s32[1,64,10]{1,0,2:T(1,128)} %param.21) | copy-start | bytes 7684
  0.6 85.0 %copy-start.7 = (f32[1,64,10]{1,0,2:T(1,128)S(1)}, f32[1,64,10]{1,0,2:T(1,128)}, u32[]{:S(2)}) copy-start(f32[1,64,10]{1,0,2:T(1,128)} %param.22) | copy-start | bytes 7684
  0.7 92.8 %copy-start.3 = (bf16[1,64,2048]{2,1,0:T(8,128)(2,1)S(1)}, bf16[1,64,2048]{2,1,0:T(8,128)(2,1)}, u32[]{:S(2)}) copy-start(bf16[1,64,2048]{2,1,0:T(8,128)(2,1)} %param.18) | copy-start | bytes 786436
  0.7 92.8 %copy-start.4 = (f32[2048]{0:T(1024)S(1)}, f32[2048]{0:T(1024)}, u32[]{:S(2)}) copy-start(f32[2048]{0:T(1024)} %param.20) | copy-start | bytes 24580
  0.7 92.8 %copy-start.5 = (f32[128]{0:T(128)S(1)}, f32[128]{0:T(128)}, u32[]{:S(2)}) copy-start(f32[128]{0:T(128)} %param.19) | copy-start | bytes 1540
  38.5 6.3 %collective-permute-start = (bf16[288,128]{1,0:T(8,128)(2,1)S(1)}, bf16[288,128]{1,0:T(8,128)(2,1)S(1)}, u32[]{:S(2)}, u32[]{:S(2)}) collective-permute-start(bf16[288,128]{1,0:T(8,128)(2,1)S(1)} %get-tuple-element.13.own_ref), channel_id=1, source_target_pairs={{0,384},{384,0},{128,256},{256,128},{1,385},{385,1},{129,257},{257... | collective-permute-start | bytes 221192 | tf_op jit(solution)/shard_map/ppermute | solution.py:596
  74.0 5.9 %collective-permute-start.1 = (f32[64,128]{1,0:T(8,128)S(1)}, f32[64,128]{1,0:T(8,128)S(1)}, u32[]{:S(2)}, u32[]{:S(2)}) collective-permute-start(f32[64,128]{1,0:T(8,128)S(1)} %fold.1.own_ref), channel_id=1, source_target_pairs={{0,384},{384,0},{128,256},{256,128},{1,385},{385,1},{129,257},{257... | collective-permute-start | bytes 98312 | tf_op jit(solution)/shard_map/ppermute | solution.py:596
  81.4 12.1 %all-to-all-start.1 = ((bf16[16,64,128]{2,1,0:T(8,128)(2,1)}), bf16[16,64,128]{2,1,0:T(8,128)(2,1)S(1)}, u32[]{:S(2)}, u32[]{:S(2)}) async-start(bf16[16,64,128]{2,1,0:T(8,128)(2,1)} %heads.1), calls=%async_computation.1 | async-start | bytes 524288 | tf_op jit(solution)/shard_map/all_to_all | solution.py:592
  96.7 112.4 %copy-start = (bf16[1,2048,256]{2,1,0:T(8,128)(2,1)S(1)}, bf16[1,2048,256]{2,1,0:T(8,128)(2,1)}, u32[]{:S(2)}) copy-start(bf16[1,2048,256]{2,1,0:T(8,128)(2,1)} %param.23) | copy-start | bytes 3145732
  96.7 112.4 %copy-start.1 = (bf16[1,2048,256]{2,1,0:T(8,128)(2,1)S(1)}, bf16[1,2048,256]{2,1,0:T(8,128)(2,1)}, u32[]{:S(2)}) copy-start(bf16[1,2048,256]{2,1,0:T(8,128)(2,1)} %param.24) | copy-start | bytes 3145732
  96.7 112.4 %copy-start.2 = (bf16[1,256,2048]{2,1,0:T(8,128)(2,1)S(1)}, bf16[1,256,2048]{2,1,0:T(8,128)(2,1)}, u32[]{:S(2)}) copy-start(bf16[1,256,2048]{2,1,0:T(8,128)(2,1)} %param.25) | copy-start | bytes 3145732

commit v5 on v4

--- a/solution.py
+++ b/solution.py
@@ -106,8 +106,26 @@
         copy.wait()
 
 
+Y_AXES = ("y4", "y2", "y1")
+HEAD_AXES = ("pair",) + Y_AXES
+SEQ_AXES = ("half",) + HEAD_AXES
+EXP_AXES = ("z4", "z2", "z1", "core")
+ROW_AXES = ("core", "half", "pair", "y1", "z1", "y2", "z2", "y4", "z4")
+OWNER_AXES = SEQ_AXES + EXP_AXES
+
+
+def reorder_bits(index, old, new):
+    moved = jnp.zeros_like(index)
+    for place, axis in enumerate(reversed(new)):
+        bit = (index >> (len(old) - 1 - old.index(axis))) & 1
+        moved = moved | (bit << place)
+    return moved
+
+
 def route_kernel(ids_ref, weight_in_ref, tok_ref, slot_ref, weight_ref):
-    expert = lax.broadcasted_iota(jnp.int32, (TOK, EXPERTS), 1)
+    expert = reorder_bits(
+        lax.broadcasted_iota(jnp.int32, (TOK, EXPERTS), 1), ROW_AXES, OWNER_AXES
+    )
     named = jnp.zeros((TOK, EXPERTS), F32)
     for k in range(TOPK):
         named = jnp.where(ids_ref[:, k : k + 1] == expert, 1.0, named)
@@ -124,7 +142,8 @@
     for k in range(TOPK):
         ids = ids_ref[:, k : k + 1]
         mine = jnp.sum(jnp.where(ids == expert, rank, 0.0), axis=1, keepdims=True)
-        slots = jnp.where(lane == k, 2 * ids + mine.astype(jnp.int32), slots)
+        place = reorder_bits(ids, OWNER_AXES, ROW_AXES)
+        slots = jnp.where(lane == k, 2 * place + mine.astype(jnp.int32), slots)
         weights = jnp.where(lane == k, weight_in_ref[:, k : k + 1], weights)
     slot_ref[:, 0:TOK] = jnp.transpose(slots.astype(F32))[0:16].astype(jnp.int32)
     slot_ref[:, TOK:128] = jnp.zeros((16, 128 - TOK), jnp.int32)
@@ -596,11 +615,6 @@
     return lax.ppermute(x, ("half", "pair"), [(0, 3), (3, 0), (1, 2), (2, 1)])
 
 
-HEAD_AXES = ("pair", "y")
-SEQ_AXES = ("half", "pair", "y")
-EXP_AXES = ("z", "core")
-
-
 def body(
     mixer_query,
     mixer_key,
@@ -631,17 +645,17 @@
     mixed, outgoing = mix(
         half, tok, heads, residual[0], out_gain.reshape(1, DH), ffn_gain.reshape(1, D)
     )
-    arrived = swap_all(outgoing, SEQ_AXES + EXP_AXES)
+    arrived = swap_all(outgoing, ROW_AXES)
     result = experts(arrived.reshape(SLOTS * 16, 128), gate_proj[0], up_proj[0], down_proj[0])
-    returned = swap_all(result.reshape(SLOTS, 16, 128), SEQ_AXES + EXP_AXES)
+    returned = swap_all(result.reshape(SLOTS, 16, 128), ROW_AXES)
     ffn_out = combine(slots, weights, returned)
     return (mixed[None], ffn_out[None])
 
 
 def solution(mesh):
-    fine = Mesh(mesh.devices.reshape(2, 2, 8, 8, 2), SEQ_AXES + EXP_AXES)
+    fine = Mesh(mesh.devices.reshape((2,) * 9), OWNER_AXES)
     rows = P(EXP_AXES, SEQ_AXES, None)
-    owned = P(SEQ_AXES + EXP_AXES, None, None)
+    owned = P(OWNER_AXES, None, None)
     return jax.shard_map(
         body,
         mesh=fine,

time: 328 us -> 331 us (level)
  blocking collectives: 279 us -> 283 us
where the time goes in v5:
time: 331 us
  blocking collectives  283 us (85%)
  Pallas kernels  25.1 us (8%)
  starting transfers between devices  11.8 us (4%)
  waiting for transfers between devices  10.2 us (3%)
    all_to_all x3, blocking collectives, swap_all(): return lax.all_to_all(x, axes, split_axis=0, concat_axis=0, tiled=True)  254 us
    all_gather x1, blocking collectives, body(): maps = lax.all_gather(compose(half, own_map, other_map), EXP_AXES, axis=0)  28.9 us
    ppermute x2, starting transfers between devices, trade(): return lax.ppermute(x, ('half', 'pair'), [(0, 3), (3, 0), (1, 2), (2, 1)])  7.56 us
    pallas_call x1, Pallas kernels, experts(): pl.pallas_call(expert_kernel, grid=(SLOTS // FFN_ROWS,), out_shape=shape(...  7.18 us
  transfers between devices with their start and end apart: 3, of which 3 were waited for; matrix products, arithmetic and copies ran while one was open for 0% of the time, Pallas kernels for 1%

profile of v5, /device:TPU:1, one launch (start us, length us, event | category | flops | bytes accessed | tf_op | source)
XLA Modules:
  0.0 330.8 jit_solution(6624739281049981369)
XLA Ops:
  0.6 0.0 copy-start.6
  0.6 0.0 copy-start.7
  0.7 0.0 copy-start.3
  0.7 0.0 copy-start.4
  0.7 0.0 copy-start.5
  0.7 1.7 pack.1
  2.4 29.8 %all_to_all.20.recv_ref = bf16[16,208,128]{2,1,0:T(8,128)(2,1)S(1)} all-to-all(bf16[16,208,128]{2,1,0:T(8,128)(2,1)S(1)} %pack.1), channel_id=1, replica_groups=mesh['half'=2,'pair'=2,'y4'=2,'y2'=2,'y1'=2,'z4'=2,'z2'=2,'z1'=2,'core'=..., dimensions={0} | all-to-all | bytes 1703936 | tf_op jit(solution)/shard_map/all_to_all | solution.py:611
  32.2 6.3 %mixer.1 = (bf16[16,64,128]{2,1,0:T(8,128)(2,1)S(1)}, f32[16,64,128]{2,1,0:T(8,128)S(1)}, f32[4,256,128]{2,1,0:T(8,128)S(1)}, f32[4,8,128]{2,1,0:T(8,128)S(1)}, bf16[288,128]{1,0:T(8,128)(2,1)S(1)}) custom-call(bf16[16,208,128]{2,1,0:T(8,128)(2,1)S(1)} %all_to_all.20.recv_ref), custom_call_target="tpu_custom_call" | custom-call | tf_op jit(solution)/shard_map/mixer/pallas_call | solution.py:510
  38.5 3.4 %collective-permute-start = (bf16[288,128]{1,0:T(8,128)(2,1)S(1)}, bf16[288,128]{1,0:T(8,128)(2,1)S(1)}, u32[]{:S(2)}, u32[]{:S(2)}) collective-permute-start(bf16[288,128]{1,0:T(8,128)(2,1)S(1)} %get-tuple-element.13.own_ref), channel_id=1, source_target_pairs={{0,384},{384,0},{128,256},{256,128},{1,385},{385,1},{129,257},{257... | collective-permute-start | bytes 221192 | tf_op jit(solution)/shard_map/ppermute | solution.py:615
  41.8 2.9 collective-permute-done.other_ref.other_map_ref
  44.8 0.2 compose.1
  44.9 28.9 %all-gather = bf16[3584,128]{1,0:T(8,128)(2,1)S(1)} all-gather(bf16[224,128]{1,0:T(8,128)(2,1)S(1)} %compose.1), channel_id=2, replica_groups=mesh['half'=2,'pair'=2,'y4'=2,'y2'=2,'y1'=2,'z4'=2,'z2'=2,'z1'=2,'core'=..., dimensions={0}, use_global_device_ids=true | all-gather | bytes 974848 | tf_op jit(solution)/shard_map/all_gather | solution.py:640
  73.8 0.1 fold.1.own_ref
  74.0 4.2 %collective-permute-start.1 = (f32[64,128]{1,0:T(8,128)S(1)}, f32[64,128]{1,0:T(8,128)S(1)}, u32[]{:S(2)}, u32[]{:S(2)}) collective-permute-start(f32[64,128]{1,0:T(8,128)S(1)} %fold.1.own_ref), channel_id=1, source_target_pairs={{0,384},{384,0},{128,256},{256,128},{1,385},{385,1},{129,257},{257... | collective-permute-start | bytes 98312 | tf_op jit(solution)/shard_map/ppermute | solution.py:615
  78.2 1.7 collective-permute-done.1.other_ref
  79.8 1.5 heads.1
  81.4 4.2 %all-to-all-start.1 = ((bf16[16,64,128]{2,1,0:T(8,128)(2,1)}), bf16[16,64,128]{2,1,0:T(8,128)(2,1)S(1)}, u32[]{:S(2)}, u32[]{:S(2)}) async-start(bf16[16,64,128]{2,1,0:T(8,128)(2,1)} %heads.1), calls=%async_computation.1 | async-start | bytes 524288 | tf_op jit(solution)/shard_map/all_to_all | solution.py:611
  85.6 0.0 copy-done.6
  85.6 0.1 copy.15
  85.7 0.0 copy-done.7
  85.7 0.1 copy.16
  85.8 2.1 route.1
  87.9 5.6 %all-to-all-done.1.heads_ref = bf16[16,64,128]{2,1,0:T(8,128)(2,1)S(1)} async-done(((bf16[16,64,128]{2,1,0:T(8,128)(2,1)}), bf16[16,64,128]{2,1,0:T(8,128)(2,1)S(1)}, u32[]{:S(2)}, u32[]{:S(2)}) %all-to-all-start.1) | async-done | bytes 262176 | tf_op jit(solution)/shard_map/all_to_all | solution.py:611
  93.5 0.0 copy-done.3
  93.5 0.0 copy-done.4
  93.5 0.0 copy-done.5
  93.5 3.2 mix.1
  96.7 0.0 copy-start
  96.7 0.0 copy-start.1
  96.7 0.0 copy-start.2
  96.7 113.9 %all_to_all.21 = bf16[1024,16,128]{2,1,0:T(8,128)(2,1)S(1)} all-to-all(bf16[1024,16,128]{2,1,0:T(8,128)(2,1)S(1)} %get-tuple-element.21), channel_id=1, replica_groups=mesh['half'=2,'pair'=2,'y4'=2,'y2'=2,'y1'=2,'z4'=2,'z2'=2,'z1'=2,'core'=..., dimensions={0} | all-to-all | bytes 8388608 | tf_op jit(solution)/shard_map/all_to_all | solution.py:611
  210.7 0.0 copy-done
  210.7 0.0 copy-done.1
  210.7 0.0 copy-done.2
  210.7 7.2 %experts.1 = bf16[16384,128]{1,0:T(8,128)(2,1)S(1)} custom-call(bf16[16384,128]{1,0:T(8,128)(2,1)S(1)} %bitcast.28, bf16[2048,256]{1,0:T(8,128)(2,1)S(1)} %bitcast.31, bf16[2048,256]{1,0:T(8,128)(2,1)S(1)} %bitcast.32, bf16[256,2048]{1,0:T(8,128)(2,1)S(1)} %bitcast.33), custom_call_target="tpu_custom_call" | custom-call | tf_op jit(solution)/shard_map/experts/pallas_call | solution.py:581
  217.9 110.1 %all_to_all.22.rows_ref = bf16[1024,16,128]{2,1,0:T(8,128)(2,1)S(1)} all-to-all(bf16[1024,16,128]{2,1,0:T(8,128)(2,1)S(1)} %bitcast.29), channel_id=1, replica_groups=mesh['half'=2,'pair'=2,'y4'=2,'y2'=2,'y1'=2,'z4'=2,'z2'=2,'z1'=2,'core'=..., dimensions={0} | all-to-all | bytes 8388608 | tf_op jit(solution)/shard_map/all_to_all | solution.py:611
  328.0 2.8 combine.1
  (1 shorter events, 0.0 us)
Async XLA Ops:
  0.6 84.9 %copy-start.6 = (s32[1,64,10]{1,0,2:T(1,128)S(1)}, s32[1,64,10]{1,0,2:T(1,128)}, u32[]{:S(2)}) copy-start(s32[1,64,10]{1,0,2:T(1,128)} %param.21) | copy-start | bytes 7684
  0.6 85.0 %copy-start.7 = (f32[1,64,10]{1,0,2:T(1,128)S(1)}, f32[1,64,10]{1,0,2:T(1,128)}, u32[]{:S(2)}) copy-start(f32[1,64,10]{1,0,2:T(1,128)} %param.22) | copy-start | bytes 7684
  0.7 92.8 %copy-start.3 = (bf16[1,64,2048]{2,1,0:T(8,128)(2,1)S(1)}, bf16[1,64,2048]{2,1,0:T(8,128)(2,1)}, u32[]{:S(2)}) copy-start(bf16[1,64,2048]{2,1,0:T(8,128)(2,1)} %param.18) | copy-start | bytes 786436
  0.7 92.8 %copy-start.4 = (f32[2048]{0:T(1024)S(1)}, f32[2048]{0:T(1024)}, u32[]{:S(2)}) copy-start(f32[2048]{0:T(1024)} %param.20) | copy-start | bytes 24580
  0.7 92.8 %copy-start.5 = (f32[128]{0:T(128)S(1)}, f32[128]{0:T(128)}, u32[]{:S(2)}) copy-start(f32[128]{0:T(128)} %param.19) | copy-start | bytes 1540
  38.5 6.3 %collective-permute-start = (bf16[288,128]{1,0:T(8,128)(2,1)S(1)}, bf16[288,128]{1,0:T(8,128)(2,1)S(1)}, u32[]{:S(2)}, u32[]{:S(2)}) collective-permute-start(bf16[288,128]{1,0:T(8,128)(2,1)S(1)} %get-tuple-element.13.own_ref), channel_id=1, source_target_pairs={{0,384},{384,0},{128,256},{256,128},{1,385},{385,1},{129,257},{257... | collective-permute-start | bytes 221192 | tf_op jit(solution)/shard_map/ppermute | solution.py:615
  74.0 5.9 %collective-permute-start.1 = (f32[64,128]{1,0:T(8,128)S(1)}, f32[64,128]{1,0:T(8,128)S(1)}, u32[]{:S(2)}, u32[]{:S(2)}) collective-permute-start(f32[64,128]{1,0:T(8,128)S(1)} %fold.1.own_ref), channel_id=1, source_target_pairs={{0,384},{384,0},{128,256},{256,128},{1,385},{385,1},{129,257},{257... | collective-permute-start | bytes 98312 | tf_op jit(solution)/shard_map/ppermute | solution.py:615
  81.4 12.1 %all-to-all-start.1 = ((bf16[16,64,128]{2,1,0:T(8,128)(2,1)}), bf16[16,64,128]{2,1,0:T(8,128)(2,1)S(1)}, u32[]{:S(2)}, u32[]{:S(2)}) async-start(bf16[16,64,128]{2,1,0:T(8,128)(2,1)} %heads.1), calls=%async_computation.1 | async-start | bytes 524288 | tf_op jit(solution)/shard_map/all_to_all | solution.py:611
  96.7 113.9 %copy-start = (bf16[1,2048,256]{2,1,0:T(8,128)(2,1)S(1)}, bf16[1,2048,256]{2,1,0:T(8,128)(2,1)}, u32[]{:S(2)}) copy-start(bf16[1,2048,256]{2,1,0:T(8,128)(2,1)} %param.23) | copy-start | bytes 3145732
  96.7 113.9 %copy-start.1 = (bf16[1,2048,256]{2,1,0:T(8,128)(2,1)S(1)}, bf16[1,2048,256]{2,1,0:T(8,128)(2,1)}, u32[]{:S(2)}) copy-start(bf16[1,2048,256]{2,1,0:T(8,128)(2,1)} %param.24) | copy-start | bytes 3145732
  96.7 113.9 %copy-start.2 = (bf16[1,256,2048]{2,1,0:T(8,128)(2,1)S(1)}, bf16[1,256,2048]{2,1,0:T(8,128)(2,1)}, u32[]{:S(2)}) copy-start(bf16[1,256,2048]{2,1,0:T(8,128)(2,1)} %param.25) | copy-start | bytes 3145732
